TPU v7x, 32 devices: a whole 2x2x4 slice. The times are simulated.
32 devices in a mesh: group: 2 (over y), ctx: 4 (over z), head: 2 (over x), req: 2 (over core).
Axes of the slice: x: 2, y: 2, z: 4, core: 2. Of those that a mesh axis runs over, the one named last changes fastest.
Arguments:
- kda_query: bfloat16 [4, 768, 4096], P(('group', 'req'), 'ctx', 'head'), parts along dimension 0, may hold values from -6 to 6
- kda_key: bfloat16 [4, 768, 4096], P(('group', 'req'), 'ctx', 'head'), parts along dimension 0, may hold values from -6 to 6
- kda_value: bfloat16 [4, 768, 4096], P(('group', 'req'), 'ctx', 'head'), parts along dimension 0, may hold values from -6 to 6
- log_decay: bfloat16 [4, 768, 4096], P(('group', 'req'), 'ctx', 'head'), parts along dimension 0, may hold values from -1 to 0
- write_strength: float32 [4, 32, 768], P(('group', 'req'), 'head', 'ctx'), parts along dimension 0, may hold values from 0.1 to 0.95
- mla_query: bfloat16 [4, 768, 18432], P(('group', 'req'), 'ctx', 'head'), parts along dimension 0, may hold values from -18 to 18
- latents: bfloat16 [4, 768, 576], P(('group', 'req'), 'ctx'), parts along dimension 0, may hold values from -8 to 8
- value_up: bfloat16 [32, 512, 128], P('head'), may hold values from -0.25 to 0.25
- out_proj: bfloat16 [4096, 2304], P('head'), may hold values from -0.09375 to 0.09375
- doc_lengths: int32 [4, 8], P(('group', 'req')), parts along dimension 0, may hold values from 1 to 288, 768 in all within a row
Outputs:
- kda_out: bfloat16 [4, 768, 4096], P(('group', 'req'), 'ctx', 'head'), parts along dimension 0
- mixed: bfloat16 [4, 768, 2304], P(('group', 'req'), ('ctx', 'head')), parts along dimension 0
There are 2 independent parts, one for each index of `group`. A program takes and returns all parts, laid end to end along the dimension named above; an argument that names none is the same for every part. Nothing has to cross between parts.
Inputs may be any that keep to these rules, and one draw needn't show every extreme that they name: `doc_lengths`: each row's lengths sum to 768, and each row's longest prompt has exactly 288 positions.
All inputs are finite; a program needn't handle non-finite values.
Results may differ from a plain program's by a relative error of at most 0.009.
Values may be sent and summed in bfloat16 or wider, within the bound.
A program may use at most 128 MiB of HBM per device.

v0:
```python
import math

import jax
import jax.numpy as jnp
from jax import lax
from jax.sharding import PartitionSpec as P

ROPE = 64
NOPE = 128
SPAN = 64


top_value = lax.Precision.HIGHEST
masked_score = -1e30


def from_behind(value, axis, by):
    peers = lax.axis_size(axis)
    pairs = [(i, i + by) for i in range(peers) if 0 <= i + by < peers]
    return lax.ppermute(value, axis, pairs)


def unit_length(values):
    return values * lax.rsqrt(jnp.sum(values * values, axis=-1, keepdims=True) + 1e-06)


def doc_index(position_list, doc_ends):
    return jnp.sum((doc_ends[None, :] <= position_list[:, None]).astype(jnp.int32), axis=1)


def span_terms(query_rows, key_rows, value_rows, decay_rows, strength, doc_ids, prev_doc):
    span_len = key_rows.shape[1]
    state_dim = key_rows.shape[2]
    row_index = jnp.arange(span_len, dtype=jnp.int32)
    inclusive = (row_index[:, None] >= row_index[None, :]).astype(jnp.float32)
    summed = jnp.einsum("ij,hjc->hic", inclusive, decay_rows, precision=top_value)
    growth = jnp.exp(summed)
    key_hat = key_rows * growth
    key_tilde = key_rows * jnp.exp(-summed)
    query_estimate = query_rows * growth
    same_doc = doc_ids[:, None] == doc_ids[None, :]
    strict = same_doc & (row_index[:, None] > row_index[None, :])
    up_to = same_doc & (row_index[:, None] >= row_index[None, :])
    carried = (doc_ids == prev_doc).astype(jnp.float32)
    inner = jnp.einsum("hic,hjc->hij", key_hat, key_tilde, precision=top_value)
    lower_part = jnp.where(strict[None], inner * strength[:, :, None], 0.0)
    system = lower_part + jnp.eye(span_len, dtype=jnp.float32)[None]
    right_side = jnp.concatenate(
        [(strength * carried[None])[:, :, None] * key_hat, strength[:, :, None] * value_rows],
        axis=2,
    )
    solved = lax.linalg.triangular_solve(
        system, right_side, left_side=True, lower=True, unit_diagonal=True
    )
    weighted_key_rows = solved[:, :, :state_dim]
    update_rows = solved[:, :, state_dim:]
    attend = jnp.where(
        up_to[None], jnp.einsum("hic,hjc->hij", query_estimate, key_tilde, precision=top_value), 0.0
    )
    tail_mask = same_doc[span_len - 1].astype(jnp.float32)
    key_decay = key_rows * jnp.exp(summed[:, span_len - 1 :, :] - summed) * tail_mask[None, :, None]
    diagonal = (
        carried[span_len - 1]
        * growth[:, span_len - 1, :, None]
        * jnp.eye(state_dim, dtype=jnp.float32)[None]
    )
    transition = diagonal - jnp.einsum(
        "hjc,hjd->hcd", key_decay, weighted_key_rows, precision=top_value
    )
    offset = jnp.einsum("hjc,hjv->hcv", key_decay, update_rows, precision=top_value)
    return (query_estimate, carried, weighted_key_rows, update_rows, attend, transition, offset)


def span_output(terms, inbound_state):
    query_estimate, carried, weighted_key_rows, update_rows, attend, transition, offset = terms
    adjusted_rows = update_rows - jnp.einsum(
        "izy,iyn->izn", weighted_key_rows, inbound_state, precision=top_value
    )
    state_contribution = jnp.einsum(
        "izy,iyn->izn", query_estimate, inbound_state, precision=top_value
    )
    return carried[None, :, None] * state_contribution + jnp.einsum(
        "hij,hjv->hiv", attend, adjusted_rows, precision=top_value
    )


def apply_map(transition, offset, inbound_state):
    return jnp.einsum("hcd,hdv->hcv", transition, inbound_state, precision=top_value) + offset


def local(
    kda_query,
    kda_key,
    kda_value,
    log_decay,
    write_strength,
    mla_query,
    latents,
    value_up,
    out_proj,
    doc_lengths,
):
    tokens_dev = kda_query.shape[1]
    heads_dev = write_strength.shape[1]
    state_dim = kda_query.shape[2] // heads_dev
    ctx_count = lax.axis_size("ctx")
    ctx_place = lax.axis_index("ctx")
    first_pos = ctx_place * tokens_dev
    positions = first_pos + jnp.arange(tokens_dev, dtype=jnp.int32)
    doc_ends = jnp.cumsum(doc_lengths[0])
    doc_ids = doc_index(positions, doc_ends)

    def head_first(packed):
        return jnp.transpose(
            packed[0].astype(jnp.float32).reshape(tokens_dev, heads_dev, state_dim), (1, 0, 2)
        )

    query_rows = unit_length(head_first(kda_query))
    key_rows = unit_length(head_first(kda_key))
    value_rows = head_first(kda_value)
    decay_rows = head_first(log_decay)
    strength = write_strength[0]
    span_list = []
    eye_batch = jnp.broadcast_to(
        jnp.eye(state_dim, dtype=jnp.float32), (heads_dev, state_dim, state_dim)
    )
    transition = eye_batch
    offset = jnp.zeros((heads_dev, state_dim, state_dim), jnp.float32)
    for span_begin in range(0, tokens_dev, SPAN):
        span_stop = span_begin + SPAN
        prev_doc = doc_index(positions[span_begin : span_begin + 1] - 1, doc_ends)[0]
        terms = span_terms(
            query_rows[:, span_begin:span_stop],
            key_rows[:, span_begin:span_stop],
            value_rows[:, span_begin:span_stop],
            decay_rows[:, span_begin:span_stop],
            strength[:, span_begin:span_stop],
            doc_ids[span_begin:span_stop],
            prev_doc,
        )
        span_list.append(terms)
        offset = apply_map(terms[5], terms[6], offset)
        transition = jnp.einsum("hcd,hde->hce", terms[5], transition, precision=top_value)

    def relay(turn_index, inbound_state):
        outgoing = apply_map(transition, offset, inbound_state)
        return from_behind(outgoing.astype(jnp.bfloat16), "ctx", 1).astype(outgoing.dtype)

    inbound_state = lax.fori_loop(0, ctx_count - 1, relay, jnp.zeros_like(offset))
    pieces = []
    state_now = inbound_state
    for span_number, terms in enumerate(span_list):
        pieces.append(span_output(terms, state_now))
        if span_number + 1 < len(span_list):
            state_now = apply_map(terms[5], terms[6], state_now)
    kda_out = (
        jnp.transpose(jnp.concatenate(pieces, axis=1), (1, 0, 2))
        .reshape(1, tokens_dev, heads_dev * state_dim)
        .astype(jnp.bfloat16)
    )
    width = latents.shape[2]
    lat_dim = value_up.shape[1]
    score_scale = 1.0 / math.sqrt(NOPE + ROPE)
    query_flat = mla_query[0].reshape(tokens_dev * heads_dev, width)
    row_pos = jnp.repeat(positions, heads_dev)
    row_doc = jnp.repeat(doc_ids, heads_dev)
    row_total_count = tokens_dev * heads_dev
    row_peak = jnp.full((row_total_count,), masked_score, jnp.float32)
    block_rows = lax.all_gather(latents, "ctx", axis=1, tiled=True)[0]
    row_count = block_rows.shape[0]
    key_pos = jnp.arange(row_count, dtype=jnp.int32)
    key_doc = doc_index(key_pos, doc_ends)
    scores = (
        lax.dot_general(
            query_flat, block_rows, (((1,), (1,)), ((), ())), preferred_element_type=jnp.float32
        )
        * score_scale
    )
    allowed = (
        (key_pos[None, :] <= row_pos[:, None])
        & (key_pos[None, :] >= 0)
        & (key_doc[None, :] == row_doc[:, None])
    )
    new_peak = jnp.maximum(row_peak, jnp.max(jnp.where(allowed, scores, masked_score), axis=1))
    exponent = jnp.where(allowed, jnp.exp(scores - new_peak[:, None]), 0.0)
    row_total = jnp.sum(exponent, axis=1)
    weighted = jnp.dot(
        exponent.astype(jnp.bfloat16), block_rows[:, :lat_dim], preferred_element_type=jnp.float32
    )
    row_peak, row_total, weighted = (new_peak, row_total, weighted)
    context = (
        (weighted / row_total[:, None]).astype(jnp.bfloat16).reshape(tokens_dev, heads_dev, lat_dim)
    )
    head_out = jnp.einsum(
        "thl,hlv->thv", context, value_up, preferred_element_type=jnp.float32
    ).astype(jnp.bfloat16)
    head_out = head_out.reshape(tokens_dev, heads_dev * value_up.shape[2])
    mixed = lax.psum_scatter(
        jnp.dot(head_out, out_proj, preferred_element_type=jnp.float32).astype(jnp.bfloat16),
        "head",
        scatter_dimension=0,
        tiled=True,
    )
    return (kda_out, mixed[None])


def solution(mesh):
    placed = (
        P(("group", "req"), "ctx", "head"),
        P(("group", "req"), "ctx", "head"),
        P(("group", "req"), "ctx", "head"),
        P(("group", "req"), "ctx", "head"),
        P(("group", "req"), "head", "ctx"),
        P(("group", "req"), "ctx", "head"),
        P(("group", "req"), "ctx", None),
        P("head", None, None),
        P("head", None),
        P(("group", "req"), None),
    )
    return jax.shard_map(
        local,
        mesh=mesh,
        in_specs=placed,
        out_specs=(P(("group", "req"), "ctx", "head"), P(("group", "req"), ("ctx", "head"), None)),
        check_vma=False,
    )
```

profile of v0, /device:TPU:0, one launch (start us, length us, event | category | flops | bytes accessed | tf_op | source)
XLA Modules:
  0.0 443.5 jit_solution(2530594987979370844)
XLA Ops:
  8.8 23.7 %all_gather.3 = bf16[1,768,576]{2,1,0:T(8,128)(2,1)S(1)} all-gather(bf16[1,192,576]{2,1,0:T(8,128)(2,1)} %param.20), channel_id=1, replica_groups=mesh['group'=2,'ctx'=4,'head'=2,'req'=2] {'ctx'}, dimensions={1}, use_global_device_ids=true | all-gather | bytes 1105920 | tf_op jit(solution)/shard_map/all_gather | solution.py:169
  32.5 7.0 %reshape_squeeze.3 = bf16[3072,576]{1,0:T(8,128)(2,1)} reshape(bf16[1,192,9216]{2,1,0:T(8,128)(2,1)} %param.19) | data formatting | bytes 7077888 | tf_op jit(solution)/shard_map/reshape;squeeze | solution.py:164
  39.4 6.7 %select_reduce_fusion = (f32[3072]{0:T(1024)S(1)}, f32[3072,768]{0,1:T(8,128)S(1)}) fusion(s32[3072]{0:T(1024)S(1)} %eq.140, s32[3072]{0:T(1024)S(1)} %le.114, s32[768]{0:T(1024)S(1)} %convert_reduce_fusion, bf16[3072,576]{1,0:T(8,128)(2,1)} %reshape_squeeze.3, bf16[1,768,576]{2,1,0:T(8,128)(2,1)S(1)} %all_gather.3), kind=kOutput, calls=%fused_computation.7 | convolution fusion | flops 2732061696 | bytes 13900800 | tf_op jit(solution)/shard_map/dot_general | solution.py:174
  46.2 3.6 fusion.6
  49.8 4.3 divide_convert_fusion
  54.2 3.7 fusion.20
  57.9 3.0 convolution_convert_fusion
  65.9 2.0 compare_convert_fusion.2
  69.7 1.3 convert_bitcast_fusion.1
  73.3 1.9 fusion.30
  75.2 80.0 %custom-call.8 = f32[16,1,64,64]{2,3,1,0:T(8,128)} custom-call(f32[16,1,64,64]{3,2,1,0:T(8,128)} %fusion.30), custom_call_target="InvertDiagBlocksLowerTriangular" | custom-call | tf_op jit(solution)/shard_map/triangular_solve/custom-call.1 | solution.py:52
  155.2 1.3 convert_bitcast_fusion
  157.8 2.8 broadcast_multiply_fusion.2
  160.6 1.4 slice_multiply_fusion.4
  163.1 1.9 fusion.68
  165.1 1.3 slice_multiply_fusion.18
  166.3 2.1 convolution_subtract_fusion
  168.4 2.1 fusion.62
  170.5 2.0 convolution_add_fusion.5
  172.4 1.9 fusion.35
  174.3 80.2 %custom-call.7 = f32[16,1,64,64]{2,3,1,0:T(8,128)} custom-call(f32[16,1,64,64]{3,2,1,0:T(8,128)} %fusion.35), custom_call_target="InvertDiagBlocksLowerTriangular" | custom-call | tf_op jit(solution)/shard_map/triangular_solve/custom-call.1 | solution.py:52
  254.5 2.4 fusion.48
  256.9 2.9 fusion.66
  259.8 3.1 convolution_subtract_fusion.1
  262.9 1.9 fusion.40
  264.7 80.2 %custom-call.6 = f32[16,1,64,64]{2,3,1,0:T(8,128)} custom-call(f32[16,1,64,64]{3,2,1,0:T(8,128)} %fusion.40), custom_call_target="InvertDiagBlocksLowerTriangular" | custom-call | tf_op jit(solution)/shard_map/triangular_solve/custom-call.1 | solution.py:52
  344.9 1.4 slice_multiply_fusion.20
  346.4 3.1 convolution_add_fusion.4
  350.6 2.1 convolution_subtract_fusion.2
  352.7 1.1 fusion.119
  353.9 3.0 convolution_add_fusion.3
  356.8 1.1 fusion.117
  358.0 2.2 fusion.118
  360.2 53.5 %while.11 = (s32[]{:T(128)}, f32[16,128,128]{2,1,0:T(8,128)S(1)}, f32[16,128,128]{2,1,0:T(8,128)}, f32[16,128,128]{2,1,0:T(8,128)}, s32[]{:T(128)}, /*index=5*/s32[]{:T(128)}) while((s32[]{:T(128)}, f32[16,128,128]{2,1,0:T(8,128)S(1)}, f32[16,128,128]{2,1,0:T(8,128)}, f32[16,128,128]{2,1,0:T(8,128)}, s32[]{:T(128)}, ...), condition=%wide.region_8.10_spmd.clone, body=%wide.region_7.9_spmd.clone.sunk | while | flops 403701760 | bytes 7340151 | solution.py:149
  360.2 3.5 fusion.158
  363.7 2.8 collective-permute-start
  366.5 9.6 %collective-permute-done = bf16[16,128,128]{2,1,0:T(8,128)(2,1)} collective-permute-done((bf16[16,128,128]{2,1,0:T(8,128)(2,1)}, bf16[16,128,128]{2,1,0:T(8,128)(2,1)}, u32[]{:S(2)}, u32[]{:S(2)}) %collective-permute-start) | collective-permute-done | bytes 524320 | tf_op jit(solution)/shard_map/while/body/eval_jaxpr/ppermute | solution.py:20
  377.3 3.5 fusion.158
  380.8 5.2 %collective-permute-start = (bf16[16,128,128]{2,1,0:T(8,128)(2,1)}, bf16[16,128,128]{2,1,0:T(8,128)(2,1)}, u32[]{:S(2)}, u32[]{:S(2)}) collective-permute-start(bf16[16,128,128]{2,1,0:T(8,128)(2,1)} %fusion.158), channel_id=1, source_target_pairs={{0,4},{4,8},{8,12},{1,5},{5,9},{9,13},{2,6},{6,10},{10,14},{3,7},{... | collective-permute-start | bytes 1572872 | tf_op jit(solution)/shard_map/while/body/eval_jaxpr/ppermute | solution.py:20
  385.9 8.7 %collective-permute-done = bf16[16,128,128]{2,1,0:T(8,128)(2,1)} collective-permute-done((bf16[16,128,128]{2,1,0:T(8,128)(2,1)}, bf16[16,128,128]{2,1,0:T(8,128)(2,1)}, u32[]{:S(2)}, u32[]{:S(2)}) %collective-permute-start) | collective-permute-done | bytes 524320 | tf_op jit(solution)/shard_map/while/body/eval_jaxpr/ppermute | solution.py:20
  395.8 3.5 fusion.158
  399.3 5.2 %collective-permute-start = (bf16[16,128,128]{2,1,0:T(8,128)(2,1)}, bf16[16,128,128]{2,1,0:T(8,128)(2,1)}, u32[]{:S(2)}, u32[]{:S(2)}) collective-permute-start(bf16[16,128,128]{2,1,0:T(8,128)(2,1)} %fusion.158), channel_id=1, source_target_pairs={{0,4},{4,8},{8,12},{1,5},{5,9},{9,13},{2,6},{6,10},{10,14},{3,7},{... | collective-permute-start | bytes 1572872 | tf_op jit(solution)/shard_map/while/body/eval_jaxpr/ppermute | solution.py:20
  404.5 7.8 %collective-permute-done = bf16[16,128,128]{2,1,0:T(8,128)(2,1)} collective-permute-done((bf16[16,128,128]{2,1,0:T(8,128)(2,1)}, bf16[16,128,128]{2,1,0:T(8,128)(2,1)}, u32[]{:S(2)}, u32[]{:S(2)}) %collective-permute-start) | collective-permute-done | bytes 524320 | tf_op jit(solution)/shard_map/while/body/eval_jaxpr/ppermute | solution.py:20
  413.7 2.4 convolution_subtract_fusion.5
  416.2 1.2 convolution_add_fusion.2
  418.9 1.2 convolution_add_fusion.1
  432.6 1.4 copy.39
  434.0 2.1 convert_element_type.184
  (128 shorter events, 29.5 us)
Async XLA Ops:
  7.2 47.0 %copy-start = (bf16[16,512,128]{2,1,0:T(8,128)(2,1)S(1)}, bf16[16,512,128]{2,1,0:T(8,128)(2,1)}, u32[]{:S(2)}) copy-start(bf16[16,512,128]{2,1,0:T(8,128)(2,1)} %param.21) | copy-start | bytes 6291460
  7.2 428.9 %reduce-scatter.2.cloned.1.call-start = ((), (), s32[]{:S(2)}) async-start(), calls=%async_computation.1 | async-start | bytes 1327104 | tf_op jit(solution)/shard_map/reduce_scatter | solution.py:198
  46.2 11.7 %slice-start = ((s8[9437184]{0:T(1024)(128)(4,1)}), s8[4194304]{0:T(1024)(128)(4,1)S(1)}, s32[]{:S(2)}) async-start(s8[9437184]{0:T(1024)(128)(4,1)} %bitcast.155), calls=%async_computation.2 | async-start | bytes 8388608
  49.8 8.1 %slice-start.1 = ((s8[9437184]{0:T(1024)(128)(4,1)}), s8[4194304]{0:T(1024)(128)(4,1)S(1)}, s32[]{:S(2)}) async-start(s8[9437184]{0:T(1024)(128)(4,1)} %bitcast.155), calls=%async_computation.3 | async-start | bytes 8388608
  49.8 8.1 %slice-start.2 = ((s8[9437184]{0:T(1024)(128)(4,1)}), s8[1048576]{0:T(1024)(128)(4,1)S(1)}, s32[]{:S(2)}) async-start(s8[9437184]{0:T(1024)(128)(4,1)} %bitcast.155), calls=%async_computation.4 | async-start | bytes 2097152
  57.9 3.6 copy-start.24
  61.7 7.9 %copy-start.28 = (f32[1,16,192]{2,1,0:T(8,128)S(1)}, f32[1,16,192]{2,1,0:T(8,128)}, u32[]{:S(2)}) copy-start(f32[1,16,192]{2,1,0:T(8,128)} %param.18) | copy-start | bytes 36868
  62.0 1.3 copy-start.21
  72.0 1.2 copy-start.2
  156.7 1.0 copy-start.3
  160.6 1.5 copy-start.26
  163.1 5.3 %copy-start.15 = (f32[16,64,256]{2,1,0:T(8,128)}, f32[16,64,256]{2,1,0:T(8,128)S(1)}, u32[]{:S(2)}) copy-start(f32[16,64,256]{2,1,0:T(8,128)S(1)} %fusion.52) | copy-start | bytes 3145732
  165.0 5.4 %copy-start.12 = (f32[16,128,128]{2,1,0:T(8,128)}, f32[16,128,128]{2,1,0:T(8,128)S(1)}, u32[]{:S(2)}) copy-start(f32[16,128,128]{2,1,0:T(8,128)S(1)} %fusion.68) | copy-start | bytes 3145732
  168.4 4.0 copy-start.8
  256.9 6.0 %copy-start.16 = (f32[16,64,256]{2,1,0:T(8,128)}, f32[16,64,256]{2,1,0:T(8,128)S(1)}, u32[]{:S(2)}) copy-start(f32[16,64,256]{2,1,0:T(8,128)S(1)} %fusion.48) | copy-start | bytes 3145732
  259.8 3.1 copy-start.5
  346.3 3.2 copy-start.22
  346.3 3.2 copy-start.23
  346.4 3.2 copy-start.27
  349.5 1.1 copy-start.6
  350.6 3.2 copy-start.18
  353.8 3.0 copy-start.10
  353.8 3.0 copy-start.20
  363.7 12.4 %collective-permute-start = (bf16[16,128,128]{2,1,0:T(8,128)(2,1)}, bf16[16,128,128]{2,1,0:T(8,128)(2,1)}, u32[]{:S(2)}, u32[]{:S(2)}) collective-permute-start(bf16[16,128,128]{2,1,0:T(8,128)(2,1)} %fusion.158), channel_id=1, source_target_pairs={{0,4},{4,8},{8,12},{1,5},{5,9},{9,13},{2,6},{6,10},{10,14},{3,7},{... | collective-permute-start | bytes 1572872 | tf_op jit(solution)/shard_map/while/body/eval_jaxpr/ppermute | solution.py:20
  380.8 13.9 %collective-permute-start = (bf16[16,128,128]{2,1,0:T(8,128)(2,1)}, bf16[16,128,128]{2,1,0:T(8,128)(2,1)}, u32[]{:S(2)}, u32[]{:S(2)}) collective-permute-start(bf16[16,128,128]{2,1,0:T(8,128)(2,1)} %fusion.158), channel_id=1, source_target_pairs={{0,4},{4,8},{8,12},{1,5},{5,9},{9,13},{2,6},{6,10},{10,14},{3,7},{... | collective-permute-start | bytes 1572872 | tf_op jit(solution)/shard_map/while/body/eval_jaxpr/ppermute | solution.py:20
  399.3 13.0 %collective-permute-start = (bf16[16,128,128]{2,1,0:T(8,128)(2,1)}, bf16[16,128,128]{2,1,0:T(8,128)(2,1)}, u32[]{:S(2)}, u32[]{:S(2)}) collective-permute-start(bf16[16,128,128]{2,1,0:T(8,128)(2,1)} %fusion.158), channel_id=1, source_target_pairs={{0,4},{4,8},{8,12},{1,5},{5,9},{9,13},{2,6},{6,10},{10,14},{3,7},{... | collective-permute-start | bytes 1572872 | tf_op jit(solution)/shard_map/while/body/eval_jaxpr/ppermute | solution.py:20
  413.7 2.4 copy-start.9
  413.7 2.4 copy-start.13
  416.2 1.2 copy-start.17
  417.4 1.2 copy-start.11
  417.4 1.5 copy-start.14
  418.9 1.2 copy-start.25
  421.3 1.0 copy-start.4
  423.4 1.2 copy-start.19
  425.7 1.3 copy-start.7
  432.5 3.6 copy-start.1
Sparse Core Ops, SparseCore 0:
  61.1 18.3 reduce-scatter.1
where the time goes:
time: 449 us; the launch traced here: 443 us
  other arithmetic  261 us (58%)
  matrix products  84.7 us (19%)
  waiting for transfers between devices  26.2 us (6%)
  blocking collectives  23.7 us (5%)
  between operations  17.1 us (4%)
  local copies, waits for them, and re-layouts  16.8 us (4%)
  starting transfers between devices  13.2 us (3%)
    another operation x5, other arithmetic, span_terms(): lax.linalg.triangular_solve(system, right_side, left_side=True, lower=Tru...  240 us
    ppermute x3, waiting for transfers between devices, from_behind(): return lax.ppermute(value, axis, pairs)  26.2 us
    all_gather x1, blocking collectives, local(): block_rows = lax.all_gather(latents, 'ctx', axis=1, tiled=True)[0]  23.7 us
    dot_general x8, matrix products, apply_map(): jnp.einsum('hcd,hdv->hcv', transition, inbound_state, precision=top_value)  19.1 us
    ppermute x3, starting transfers between devices, from_behind(): return lax.ppermute(value, axis, pairs)  13.1 us
  transfers between devices with their start and end apart: 4, of which 3 were waited for; matrix products, arithmetic and copies ran while one was open for 75% of the time, Pallas kernels for 0%

commit v1 on v0

v1 whole, which is shorter than its diff:
```python
import functools
import math

import jax
import jax.numpy as jnp
from jax import lax
from jax.experimental import pallas as pl
from jax.experimental.pallas import tpu as pltpu
from jax.sharding import PartitionSpec as P

ROPE = 64
NOPE = 128
SPAN = 64
HEADS_STEP = 4

masked_score = -1e30
ROWS = (((1,), (0,)), ((), ()))
TRANS = (((1,), (1,)), ((), ()))
OVER = (((0,), (0,)), ((), ()))


def from_behind(value, axis, by):
    peers = lax.axis_size(axis)
    pairs = [(i, i + by) for i in range(peers) if 0 <= i + by < peers]
    return lax.ppermute(value, axis, pairs)


def doc_index(position_list, doc_ends):
    return jnp.sum((doc_ends[None, :] <= position_list[:, None]).astype(jnp.int32), axis=1)


def dot_once(left, right, dims):
    return lax.dot_general(
        left.astype(jnp.bfloat16),
        right.astype(jnp.bfloat16),
        dims,
        preferred_element_type=jnp.float32,
    )


def halves(value):
    high = value.astype(jnp.bfloat16)
    return high, (value - high.astype(jnp.float32)).astype(jnp.bfloat16)


def dot_split(left, right, dims):
    left_high, left_low = halves(left)
    right_high, right_low = halves(right)
    return (
        dot_once(left_high, right_low, dims) + dot_once(left_low, right_high, dims)
    ) + dot_once(left_high, right_high, dims)


def delta_terms(
    query_ref,
    key_ref,
    value_ref,
    decay_ref,
    strength_ref,
    doc_col_ref,
    doc_row_ref,
    carried_ref,
    readout_ref,
    local_ref,
    transition_ref,
    offset_ref,
):
    tokens = query_ref.shape[1]
    state_dim = transition_ref.shape[1]
    spans = tokens // SPAN
    heads = range(strength_ref.shape[2])
    row = lax.broadcasted_iota(jnp.int32, (tokens, tokens), 0)
    col = lax.broadcasted_iota(jnp.int32, (tokens, tokens), 1)
    inclusive = jnp.where(row >= col, 1.0, 0.0).astype(jnp.bfloat16)
    same_doc = doc_col_ref[...] == doc_row_ref[...]
    strict = same_doc & (row > col)
    up_to = same_doc & (row >= col)
    carried = carried_ref[:, 0:1]
    tail = jnp.where(doc_col_ref[...] == doc_col_ref[tokens - 1 : tokens, :], 1.0, 0.0)
    small_row = lax.broadcasted_iota(jnp.int32, (SPAN, SPAN), 0)
    small_col = lax.broadcasted_iota(jnp.int32, (SPAN, SPAN), 1)
    queries, keys, strengths, summed = [], [], [], []
    for h in heads:
        lanes = slice(h * state_dim, (h + 1) * state_dim)
        query = query_ref[0, :, lanes].astype(jnp.float32)
        key = key_ref[0, :, lanes].astype(jnp.float32)
        queries.append(query * lax.rsqrt(jnp.sum(query * query, axis=1, keepdims=True) + 1e-06))
        keys.append(key * lax.rsqrt(jnp.sum(key * key, axis=1, keepdims=True) + 1e-06))
        strengths.append(strength_ref[0, :, h : h + 1])
        summed.append(dot_once(inclusive, decay_ref[0, :, lanes], ROWS))
    attends, lowers = [], []
    for h in heads:
        attend_rows, lower_rows = [], []
        for a in range(spans):
            here = slice(a * SPAN, (a + 1) * SPAN)
            seen = (a + 1) * SPAN
            if a == 0:
                start = jnp.zeros((1, state_dim), jnp.float32)
            else:
                start = summed[h][a * SPAN - 1 : a * SPAN]
            fall = jnp.exp(summed[h][here] - start)
            stacked = jnp.concatenate([keys[h][here] * fall, queries[h][here] * fall], axis=0)
            lifted = keys[h][:seen] * jnp.exp(start - summed[h][:seen])
            both = dot_split(stacked, lifted, TRANS)
            lower_rows.append(
                jnp.where(strict[here, :seen], both[:SPAN] * strengths[h][here], 0.0)
            )
            attend_rows.append(jnp.where(up_to[here, :seen], both[SPAN:], 0.0))
        attends.append(attend_rows)
        lowers.append(lower_rows)
    inverses = [[None] * spans for _ in heads]
    width = 1
    while width < SPAN:
        corner = (small_row // (2 * width) == small_col // (2 * width)) & (
            small_row // width > small_col // width
        )
        cells = [(h, a) for h in heads for a in range(spans)]
        parts = {
            (h, a): jnp.where(corner, lowers[h][a][:, a * SPAN :], 0.0) for h, a in cells
        }
        if width == 1:
            for h, a in cells:
                inverses[h][a] = -parts[h, a]
        else:
            lefts = {
                (h, a): parts[h, a] + dot_once(inverses[h][a], parts[h, a], ROWS)
                for h, a in cells
            }
            for h, a in cells:
                inverses[h][a] = inverses[h][a] - (
                    lefts[h, a] + dot_once(lefts[h, a], inverses[h][a], ROWS)
                )
        width *= 2
    solved = [[] for _ in heads]
    growths = [jnp.exp(summed[h]) for h in heads]
    for a in range(spans):
        here = slice(a * SPAN, (a + 1) * SPAN)
        for h in heads:
            lanes = slice(h * state_dim, (h + 1) * state_dim)
            right = strengths[h][here] * jnp.concatenate(
                [
                    carried[here] * keys[h][here] * growths[h][here],
                    value_ref[0, here, lanes].astype(jnp.float32),
                ],
                axis=1,
            )
            if a > 0:
                before = jnp.concatenate(solved[h], axis=0) if a > 1 else solved[h][0]
                right = right - dot_once(lowers[h][a][:, : a * SPAN], before, ROWS)
            solved[h].append(right + dot_once(inverses[h][a], right, ROWS))
    eye = jnp.where(
        lax.broadcasted_iota(jnp.int32, (state_dim, state_dim), 0)
        == lax.broadcasted_iota(jnp.int32, (state_dim, state_dim), 1),
        1.0,
        0.0,
    )
    for h in heads:
        lanes = slice(h * state_dim, (h + 1) * state_dim)
        whole = jnp.concatenate(solved[h], axis=0)
        whole_halves = halves(whole)
        for a in range(spans):
            here = slice(a * SPAN, (a + 1) * SPAN)
            seen = (a + 1) * SPAN
            attend_high, attend_low = halves(attends[h][a])
            read = (
                dot_once(attend_high, whole_halves[1][:seen], ROWS)
                + dot_once(attend_low, whole_halves[0][:seen], ROWS)
            ) + dot_once(attend_high, whole_halves[0][:seen], ROWS)
            readout_ref[here, lanes] = (
                carried[here] * queries[h][here] * growths[h][here] - read[:, :state_dim]
            ).astype(readout_ref.dtype)
            local_ref[here, lanes] = read[:, state_dim:]
        last = summed[h][tokens - 1 : tokens]
        key_decay = keys[h] * jnp.exp(last - summed[h]) * tail
        moved = dot_split(key_decay, whole, OVER)
        kept = carried[tokens - 1 : tokens] * growths[h][tokens - 1 : tokens]
        transition_ref[h] = (eye * kept - moved[:, :state_dim]).astype(transition_ref.dtype)
        offset_ref[h] = moved[:, state_dim:]


def delta_readout(readout_ref, local_ref, state_ref, out_ref):
    state_dim = state_ref.shape[1]
    for h in range(state_ref.shape[0]):
        lanes = slice(h * state_dim, (h + 1) * state_dim)
        out_ref[0, :, lanes] = (
            local_ref[:, lanes]
            + jnp.dot(readout_ref[:, lanes], state_ref[h], preferred_element_type=jnp.float32)
        ).astype(out_ref.dtype)


def local(
    kda_query,
    kda_key,
    kda_value,
    log_decay,
    write_strength,
    mla_query,
    latents,
    value_up,
    out_proj,
    doc_lengths,
):
    tokens_dev = kda_query.shape[1]
    heads_dev = write_strength.shape[1]
    state_dim = kda_query.shape[2] // heads_dev
    ctx_count = lax.axis_size("ctx")
    ctx_place = lax.axis_index("ctx")
    longest = 3 * tokens_dev * ctx_count // 8
    hops = min(ctx_count - 1, -(-(longest - 1) // tokens_dev))
    first_pos = ctx_place * tokens_dev
    positions = first_pos + jnp.arange(tokens_dev, dtype=jnp.int32)
    doc_ends = jnp.cumsum(doc_lengths[0])
    doc_ids = doc_index(positions, doc_ends)
    prev_doc = doc_index(first_pos[None] - 1, doc_ends)
    carried = (doc_ids == prev_doc).astype(jnp.float32)

    window = [from_behind(latents[0], "ctx", by) for by in range(hops, 0, -1)]
    block_rows = jnp.concatenate(window + [latents[0]], axis=0)

    steps = heads_dev // HEADS_STEP
    lanes_step = HEADS_STEP * state_dim
    strength = jnp.transpose(
        write_strength[0].reshape(steps, HEADS_STEP, tokens_dev), (0, 2, 1)
    )
    packed = pl.BlockSpec((1, tokens_dev, lanes_step), lambda i: (0, 0, i))
    flat = pl.BlockSpec((tokens_dev, lanes_step), lambda i: (0, i))
    column = pl.BlockSpec((tokens_dev, 1), lambda i: (0, 0))
    square = pl.BlockSpec((HEADS_STEP, state_dim, state_dim), lambda i: (i, 0, 0))
    readout, local_part, transition, offset = pl.pallas_call(
        delta_terms,
        grid=(steps,),
        in_specs=[packed] * 4
        + [
            pl.BlockSpec((1, tokens_dev, HEADS_STEP), lambda i: (i, 0, 0)),
            column,
            pl.BlockSpec((1, tokens_dev), lambda i: (0, 0)),
            column,
        ],
        out_specs=[flat, flat, square, square],
        out_shape=[
            jax.ShapeDtypeStruct((tokens_dev, heads_dev * state_dim), jnp.bfloat16),
            jax.ShapeDtypeStruct((tokens_dev, heads_dev * state_dim), jnp.float32),
            jax.ShapeDtypeStruct((heads_dev, state_dim, state_dim), jnp.bfloat16),
            jax.ShapeDtypeStruct((heads_dev, state_dim, state_dim), jnp.float32),
        ],
        compiler_params=pltpu.CompilerParams(vmem_limit_bytes=48 << 20),
        cost_estimate=pl.CostEstimate(
            flops=20_000_000_000, bytes_accessed=8_000_000, transcendentals=0
        ),
    )(
        kda_query,
        kda_key,
        kda_value,
        log_decay,
        strength,
        doc_ids[:, None],
        doc_ids[None, :],
        carried[:, None],
    )

    inbound_state = None
    for hop in range(hops):
        outgoing = offset
        if hop > 0:
            outgoing = offset + jnp.einsum(
                "hcd,hdv->hcv", transition, inbound_state, preferred_element_type=jnp.float32
            )
        inbound_state = from_behind(outgoing.astype(jnp.bfloat16), "ctx", 1)
    kda_out = pl.pallas_call(
        delta_readout,
        grid=(steps,),
        in_specs=[flat, flat, square],
        out_specs=packed,
        out_shape=jax.ShapeDtypeStruct((1, tokens_dev, heads_dev * state_dim), jnp.bfloat16),
        cost_estimate=pl.CostEstimate(
            flops=100_000_000, bytes_accessed=4_000_000, transcendentals=0
        ),
    )(readout, local_part, inbound_state)

    width = latents.shape[2]
    lat_dim = value_up.shape[1]
    score_scale = 1.0 / math.sqrt(NOPE + ROPE)
    query_flat = mla_query[0].reshape(tokens_dev * heads_dev, width)
    row_pos = jnp.repeat(positions, heads_dev)
    row_doc = jnp.repeat(doc_ids, heads_dev)
    row_total_count = tokens_dev * heads_dev
    row_peak = jnp.full((row_total_count,), masked_score, jnp.float32)
    row_count = block_rows.shape[0]
    key_pos = first_pos - hops * tokens_dev + jnp.arange(row_count, dtype=jnp.int32)
    key_doc = doc_index(key_pos, doc_ends)
    scores = (
        lax.dot_general(
            query_flat, block_rows, (((1,), (1,)), ((), ())), preferred_element_type=jnp.float32
        )
        * score_scale
    )
    allowed = (
        (key_pos[None, :] <= row_pos[:, None])
        & (key_pos[None, :] >= 0)
        & (key_doc[None, :] == row_doc[:, None])
    )
    new_peak = jnp.maximum(row_peak, jnp.max(jnp.where(allowed, scores, masked_score), axis=1))
    exponent = jnp.where(allowed, jnp.exp(scores - new_peak[:, None]), 0.0)
    row_total = jnp.sum(exponent, axis=1)
    weighted = jnp.dot(
        exponent.astype(jnp.bfloat16), block_rows[:, :lat_dim], preferred_element_type=jnp.float32
    )
    row_peak, row_total, weighted = (new_peak, row_total, weighted)
    context = (
        (weighted / row_total[:, None]).astype(jnp.bfloat16).reshape(tokens_dev, heads_dev, lat_dim)
    )
    head_out = jnp.einsum(
        "thl,hlv->thv", context, value_up, preferred_element_type=jnp.float32
    ).astype(jnp.bfloat16)
    head_out = head_out.reshape(tokens_dev, heads_dev * value_up.shape[2])
    mixed = lax.psum_scatter(
        jnp.dot(head_out, out_proj, preferred_element_type=jnp.float32).astype(jnp.bfloat16),
        "head",
        scatter_dimension=0,
        tiled=True,
    )
    return (kda_out, mixed[None])


def solution(mesh):
    placed = (
        P(("group", "req"), "ctx", "head"),
        P(("group", "req"), "ctx", "head"),
        P(("group", "req"), "ctx", "head"),
        P(("group", "req"), "ctx", "head"),
        P(("group", "req"), "head", "ctx"),
        P(("group", "req"), "ctx", "head"),
        P(("group", "req"), "ctx", None),
        P("head", None, None),
        P("head", None),
        P(("group", "req"), None),
    )
    return jax.shard_map(
        local,
        mesh=mesh,
        in_specs=placed,
        out_specs=(P(("group", "req"), "ctx", "head"), P(("group", "req"), ("ctx", "head"), None)),
        check_vma=False,
    )
```

time: 449 us -> 113 us (0.25)
  other arithmetic: 261 us -> 6.2 us
  matrix products: 84.7 us -> 17.6 us
  blocking collectives: 23.7 us -> 0 us
  Pallas kernels: 0 us -> 20 us
  starting transfers between devices: 13.2 us -> 19.9 us
  local copies, waits for them, and re-layouts: 16.8 us -> 11.9 us
    another operation x6 -> x1, other arithmetic: 241 us -> 0.83 us  [the longest x5 240 us: span_terms(): lax.linalg.triangular_solve(system, right_side, left_side=True, lower=Tru...]
    dot_general x35 -> x1, matrix products: 62.4 us -> 0.29 us  [local(): jnp.einsum('hcd,hdv->hcv', transition, inbound_state, preferred_element_t...]
    all_gather x1 -> x0, blocking collectives: 23.7 us -> none  [local(): block_rows = lax.all_gather(latents, 'ctx', axis=1, tiled=True)[0]]
    pallas_call x0 -> x2, Pallas kernels: none -> 20 us  [the longest x1 16 us: local(): pl.pallas_call(delta_terms, grid=(steps,), in_specs=[packed] * 4 + [pl.Bl...]
    ppermute x3 -> x4, starting transfers between devices: 13.1 us -> 19.9 us  [from_behind(): return lax.ppermute(value, axis, pairs)]
    mul x6 -> x0, other arithmetic: 5.7 us -> none  [the longest x2 2.66 us: span_terms(): carried[span_len - 1] * growth[:, span_len - 1, :, None]]
    convert_element_type x9 -> x2, other arithmetic: 5.5 us -> 0.74 us  [the longest x1 0.66 us: local(): carried = (doc_ids == prev_doc).astype(jnp.float32)]
    another operation x3 -> x0, matrix products: 4.56 us -> none  [span_terms(): lax.linalg.triangular_solve(system, right_side, left_side=True, lower=Tru...]
  transfers between devices with their start and end apart: 4 -> 5, of which waited for: 3 -> 2; matrix products, arithmetic and copies ran while one was open for 75% -> 9% of each run, Pallas kernels for 0% -> 18%
where the time goes in v1:
time: 113 us; the launch traced here: 112 us
  waiting for transfers between devices  21.8 us (19%)
  Pallas kernels  20 us (18%)
  starting transfers between devices  19.9 us (18%)
  matrix products  17.6 us (16%)
  between operations  14.3 us (13%)
  local copies, waits for them, and re-layouts  11.9 us (11%)
  other arithmetic  6.2 us (5%)
    ppermute x4, waiting for transfers between devices, from_behind(): return lax.ppermute(value, axis, pairs)  21.8 us
    ppermute x4, starting transfers between devices, from_behind(): return lax.ppermute(value, axis, pairs)  19.9 us
    pallas_call x1, Pallas kernels, local(): pl.pallas_call(delta_terms, grid=(steps,), in_specs=[packed] * 4 + [pl.Bl...  16 us
    another operation x1, local copies, waits for them, and re-layouts, local(): query_flat = mla_query[0].reshape(tokens_dev * heads_dev, width)  6.97 us
    dot_general x1, matrix products, local(): lax.dot_general(query_flat, block_rows, (((1,), (1,)), ((), ())), preferr...  5.96 us
    dot_general x1, matrix products, local(): jnp.dot(exponent.astype(jnp.bfloat16), block_rows[:, :lat_dim], preferred...  4.55 us
    unnamed x24, local copies, waits for them, and re-layouts  4.24 us
    pallas_call x1, Pallas kernels, local(): pl.pallas_call(delta_readout, grid=(steps,), in_specs=[flat, flat, square...  4.02 us
  transfers between devices with their start and end apart: 5, of which 2 were waited for; matrix products, arithmetic and copies ran while one was open for 9% of the time, Pallas kernels for 18%

profile of v1, /device:TPU:0, one launch (start us, length us, event | category | flops | bytes accessed | tf_op | source)
XLA Modules:
  0.0 111.7 jit_solution(12744050901525102015)
XLA Ops:
  7.2 0.0 copy-start
  7.2 0.0 reduce-scatter.2.cloned.1.call-start
  7.2 6.1 %collective-permute-start.2 = (bf16[192,576]{1,0:T(8,128)(2,1)}, bf16[192,576]{1,0:T(8,128)(2,1)S(1)}, u32[]{:S(2)}, u32[]{:S(2)}) collective-permute-start(bf16[192,576]{1,0:T(8,128)(2,1)} %bitcast.43), channel_id=1, source_target_pairs={{0,8},{4,12},{1,9},{5,13},{2,10},{6,14},{3,11},{7,15},{16,24},{20,... | collective-permute-start | bytes 663560 | tf_op jit(solution)/shard_map/ppermute | solution.py:25
  13.3 3.5 %collective-permute-start.3 = (bf16[192,576]{1,0:T(8,128)(2,1)}, bf16[192,576]{1,0:T(8,128)(2,1)S(1)}, u32[]{:S(2)}, u32[]{:S(2)}) collective-permute-start(bf16[192,576]{1,0:T(8,128)(2,1)} %bitcast.44), channel_id=1, source_target_pairs={{0,4},{4,8},{8,12},{1,5},{5,9},{9,13},{2,6},{6,10},{10,14},{3,7},{... | collective-permute-start | bytes 663560 | tf_op jit(solution)/shard_map/ppermute | solution.py:25
  16.9 0.8 reduce-window.4
  17.7 0.1 convert_reduce_fusion
  17.8 0.1 convert_reduce_fusion.1
  17.9 0.1 broadcast_in_dim.41
  18.0 0.0 copy-start.7
  18.0 0.1 eq.33
  18.1 0.1 broadcast_in_dim.40
  18.2 0.1 le.67
  18.3 0.0 copy-start.8
  18.3 7.0 %reshape_squeeze.7 = bf16[3072,576]{1,0:T(8,128)(2,1)} reshape(bf16[1,192,9216]{2,1,0:T(8,128)(2,1)} %param.15) | data formatting | bytes 7077888 | tf_op jit(solution)/shard_map/reshape;squeeze | solution.py:283
  25.2 0.1 copy.26.doc_col_ref
  25.4 0.6 fusion.34
  26.0 0.0 copy-done.7
  26.0 0.2 copy.23
  26.2 0.7 compare_convert_fusion.carried_ref
  26.9 0.0 collective-permute-done.2
  26.9 0.0 collective-permute-done.3
  26.9 0.0 copy-done.8
  26.9 6.0 %fusion = (f32[3072]{0:T(1024)S(1)}, f32[576,3072]{1,0:T(8,128)S(1)}) fusion(s32[3072]{0:T(1024)S(1)} %eq.33, s32[576]{0:T(1024)S(1)} %convert_reduce_fusion, pred[576]{0:T(1024)(128)(4,1)S(1)} %broadcast_compare_fusion, s32[3072]{0:T(1024)S(1)} %le.67, s32[576]{0:T(1024)S(1)} %iota_add_fusion, bf16[3072,576]{1,0:T(8,128)(2,1)} %reshape_squeeze.7, ...), kind=kOutput, calls=%fused_computation.2 | convolution fusion | flops 2052805632 | bytes 11322432 | tf_op jit(solution)/shard_map/dot_general | solution.py:292
  32.9 0.0 slice-start
  32.9 3.8 %fusion.3 = f32[3072]{0:T(1024)S(1)} fusion(f32[576,3072]{1,0:T(8,128)S(1)} %get-tuple-element.11, f32[3072]{0:T(1024)S(1)} %broadcast_maximum_fusion, s32[3072]{0:T(1024)S(1)} %eq.33, s32[576]{0:T(1024)S(1)} %convert_reduce_fusion, pred[576]{0:T(1024)(128)(4,1)S(1)} %broadcast_compare_fusion, s32[3072]{0:T(1024)S(1)} %le.67, s32[576]{0:T(1024)S(1)} %iota_add_fusion), kind=kLoop, calls=%fused_computation.7 | loop fusion | flops 14152704 | bytes 7132224 | tf_op jit(solution)/shard_map/reduce_sum | solution.py:304
  36.7 0.0 slice-start.1
  36.7 0.0 slice-start.2
  36.7 4.5 %divide_convert_fusion = bf16[3072,512]{1,0:T(8,128)(2,1)S(1)} fusion(f32[3072]{0:T(1024)S(1)} %fusion.3, f32[576,3072]{1,0:T(8,128)S(1)} %get-tuple-element.11, f32[3072]{0:T(1024)S(1)} %broadcast_maximum_fusion, bf16[192,576]{1,0:T(8,128)(2,1)S(1)} %bitcast.46, bf16[192,576]{1,0:T(8,128)(2,1)S(1)} %collective-permute-done.3, ...), kind=kOutput, calls=%fused_computation.6 | convolution fusion | flops 1831010304 | bytes 10941504 | tf_op jit(solution)/shard_map/dot_general | solution.py:305
  41.3 0.0 copy-done
  41.3 3.7 %fusion.18 = bf16[16,24,8,128]{3,2,1,0:T(8,128)(2,1)S(1)} fusion(bf16[16,512,128]{2,1,0:T(8,128)(2,1)S(1)} %copy-done, bf16[192,16,512]{2,1,0:T(8,128)(2,1)S(1)} %bitcast.48), kind=kOutput, calls=%fused_computation.19 | convolution fusion | flops 403046400 | bytes 6029312 | tf_op jit(solution)/shard_map/thl,hlv->thv/dot_general | solution.py:312
  45.0 0.0 slice-done
  45.1 0.0 copy-start.2
  45.1 3.0 %convolution_convert_fusion = bf16[192,2304]{1,0:T(8,128)(2,1)} fusion(bf16[2048,2304]{1,0:T(8,128)(2,1)S(1)} %bitcast.41, bf16[16,24,8,128]{3,2,1,0:T(8,128)(2,1)S(1)} %fusion.18), kind=kOutput, calls=%fused_computation.9 | convolution fusion | flops 1812381696 | bytes 11108352 | tf_op jit(solution)/shard_map/dot_general | solution.py:317
  48.1 0.0 reduce-scatter.2.cloned.1.call-update
  48.2 0.0 copy-start.3
  48.2 1.1 %copy-done.3 = bf16[1,192,2048]{2,1,0:T(8,128)(2,1)S(1)} copy-done((bf16[1,192,2048]{2,1,0:T(8,128)(2,1)S(1)}, bf16[1,192,2048]{2,1,0:T(8,128)(2,1)}, u32[]{:S(2)}) %copy-start.3) | copy-done | bytes 786456
  49.3 1.1 %copy-done.4 = bf16[1,192,2048]{2,1,0:T(8,128)(2,1)S(1)} copy-done((bf16[1,192,2048]{2,1,0:T(8,128)(2,1)S(1)}, bf16[1,192,2048]{2,1,0:T(8,128)(2,1)}, u32[]{:S(2)}) %copy-start.4) | copy-done | bytes 786456
  50.4 1.1 %copy-done.5 = bf16[1,192,2048]{2,1,0:T(8,128)(2,1)S(1)} copy-done((bf16[1,192,2048]{2,1,0:T(8,128)(2,1)S(1)}, bf16[1,192,2048]{2,1,0:T(8,128)(2,1)}, u32[]{:S(2)}) %copy-start.5) | copy-done | bytes 786456
  51.6 16.0 %shard_map.113 = (bf16[192,2048]{1,0:T(8,128)(2,1)S(1)}, f32[192,2048]{1,0:T(8,128)}, bf16[16,128,128]{2,1,0:T(8,128)(2,1)S(1)}, f32[16,128,128]{2,1,0:T(8,128)S(1)}) custom-call(bf16[1,192,2048]{2,1,0:T(8,128)(2,1)S(1)} %copy-done.2, bf16[1,192,2048]{2,1,0:T(8,128)(2,1)S(1)} %copy-done.3, bf16[1,192,2048]{2,1,0:T(8,128)(2,1)S(1)} %copy-done.4, ...), custom_call_target="tpu_custom_call" | custom-call | flops 20000000000 | bytes 8000000 | tf_op jit(solution)/shard_map/pallas_call | solution.py:229
  67.5 0.1 convert_element_type.52
  67.6 5.9 %collective-permute-start = (bf16[16,128,128]{2,1,0:T(8,128)(2,1)S(1)}, bf16[16,128,128]{2,1,0:T(8,128)(2,1)S(1)}, u32[]{:S(2)}, u32[]{:S(2)}) collective-permute-start(bf16[16,128,128]{2,1,0:T(8,128)(2,1)S(1)} %convert_element_type.52), channel_id=1, source_target_pairs={{0,4},{4,8},{8,12},{1,5},{5,9},{9,13},{2,6},{6,10},{10,14},{3,7},{... | collective-permute-start | bytes 1572872 | tf_op jit(solution)/shard_map/ppermute | solution.py:25
  73.5 11.3 %collective-permute-done = bf16[16,128,128]{2,1,0:T(8,128)(2,1)S(1)} collective-permute-done((bf16[16,128,128]{2,1,0:T(8,128)(2,1)S(1)}, bf16[16,128,128]{2,1,0:T(8,128)(2,1)S(1)}, u32[]{:S(2)}, u32[]{:S(2)}) %collective-permute-start) | collective-permute-done | bytes 524320 | tf_op jit(solution)/shard_map/ppermute | solution.py:25
  84.8 0.3 fusion.17
  85.1 0.0 copy-done.1
  85.1 4.4 %collective-permute-start.1 = (bf16[16,128,128]{2,1,0:T(8,128)(2,1)S(1)}, bf16[16,128,128]{2,1,0:T(8,128)(2,1)S(1)}, u32[]{:S(2)}, u32[]{:S(2)}) collective-permute-start(bf16[16,128,128]{2,1,0:T(8,128)(2,1)S(1)} %fusion.17), channel_id=1, source_target_pairs={{0,4},{4,8},{8,12},{1,5},{5,9},{9,13},{2,6},{6,10},{10,14},{3,7},{... | collective-permute-start | bytes 1572872 | tf_op jit(solution)/shard_map/ppermute | solution.py:25
  89.6 10.5 %collective-permute-done.1.state_ref = bf16[16,128,128]{2,1,0:T(8,128)(2,1)S(1)} collective-permute-done((bf16[16,128,128]{2,1,0:T(8,128)(2,1)S(1)}, bf16[16,128,128]{2,1,0:T(8,128)(2,1)S(1)}, u32[]{:S(2)}, u32[]{:S(2)}) %collective-permute-start.1) | collective-permute-done | bytes 524320 | tf_op jit(solution)/shard_map/ppermute | solution.py:25
  100.0 0.8 copy-done.6
  100.8 4.0 %shard_map.114 = bf16[1,192,2048]{2,1,0:T(8,128)(2,1)} custom-call(bf16[192,2048]{1,0:T(8,128)(2,1)} %copy-done.1, f32[192,2048]{1,0:T(8,128)} %get-tuple-element.7.local_ref, bf16[16,128,128]{2,1,0:T(8,128)(2,1)} %copy-done.6), custom_call_target="tpu_custom_call" | custom-call | flops 100000000 | bytes 4000000 | tf_op jit(solution)/shard_map/pallas_call | solution.py:269
  (14 shorter events, 0.0 us)
Async XLA Ops:
  7.2 34.1 %copy-start = (bf16[16,512,128]{2,1,0:T(8,128)(2,1)S(1)}, bf16[16,512,128]{2,1,0:T(8,128)(2,1)}, u32[]{:S(2)}) copy-start(bf16[16,512,128]{2,1,0:T(8,128)(2,1)} %param.17) | copy-start | bytes 6291460
  7.2 97.7 %reduce-scatter.2.cloned.1.call-start = ((), (), s32[]{:S(2)}) async-start(), calls=%async_computation.1 | async-start | bytes 1327104 | tf_op jit(solution)/shard_map/reduce_scatter | solution.py:316
  7.2 19.7 %collective-permute-start.2 = (bf16[192,576]{1,0:T(8,128)(2,1)}, bf16[192,576]{1,0:T(8,128)(2,1)S(1)}, u32[]{:S(2)}, u32[]{:S(2)}) collective-permute-start(bf16[192,576]{1,0:T(8,128)(2,1)} %bitcast.43), channel_id=1, source_target_pairs={{0,8},{4,12},{1,9},{5,13},{2,10},{6,14},{3,11},{7,15},{16,24},{20,... | collective-permute-start | bytes 663560 | tf_op jit(solution)/shard_map/ppermute | solution.py:25
  13.3 13.6 %collective-permute-start.3 = (bf16[192,576]{1,0:T(8,128)(2,1)}, bf16[192,576]{1,0:T(8,128)(2,1)S(1)}, u32[]{:S(2)}, u32[]{:S(2)}) collective-permute-start(bf16[192,576]{1,0:T(8,128)(2,1)} %bitcast.44), channel_id=1, source_target_pairs={{0,4},{4,8},{8,12},{1,5},{5,9},{9,13},{2,6},{6,10},{10,14},{3,7},{... | collective-permute-start | bytes 663560 | tf_op jit(solution)/shard_map/ppermute | solution.py:25
  18.0 8.0 %copy-start.7 = (f32[1,16,192]{2,1,0:T(8,128)S(1)}, f32[1,16,192]{2,1,0:T(8,128)}, u32[]{:S(2)}) copy-start(f32[1,16,192]{2,1,0:T(8,128)} %param.14) | copy-start | bytes 36868
  18.3 8.6 %copy-start.8 = (bf16[1,192,576]{2,1,0:T(8,128)(2,1)S(1)}, bf16[1,192,576]{2,1,0:T(8,128)(2,1)}, u32[]{:S(2)}) copy-start(bf16[1,192,576]{2,1,0:T(8,128)(2,1)} %param.16) | copy-start | bytes 663556
  32.9 12.1 %slice-start = ((s8[9437184]{0:T(1024)(128)(4,1)}), s8[4194304]{0:T(1024)(128)(4,1)S(1)}, s32[]{:S(2)}) async-start(s8[9437184]{0:T(1024)(128)(4,1)} %bitcast.40), calls=%async_computation.2 | async-start | bytes 8388608
  36.7 8.3 %slice-start.1 = ((s8[9437184]{0:T(1024)(128)(4,1)}), s8[4194304]{0:T(1024)(128)(4,1)S(1)}, s32[]{:S(2)}) async-start(s8[9437184]{0:T(1024)(128)(4,1)} %bitcast.40), calls=%async_computation.3 | async-start | bytes 8388608
  36.7 8.3 %slice-start.2 = ((s8[9437184]{0:T(1024)(128)(4,1)}), s8[1048576]{0:T(1024)(128)(4,1)S(1)}, s32[]{:S(2)}) async-start(s8[9437184]{0:T(1024)(128)(4,1)} %bitcast.40), calls=%async_computation.4 | async-start | bytes 2097152
  45.1 3.1 %copy-start.2 = (bf16[1,192,2048]{2,1,0:T(8,128)(2,1)S(1)}, bf16[1,192,2048]{2,1,0:T(8,128)(2,1)}, u32[]{:S(2)}) copy-start(bf16[1,192,2048]{2,1,0:T(8,128)(2,1)} %query_ref.1) | copy-start | bytes 2359300
  48.2 1.1 %copy-start.3 = (bf16[1,192,2048]{2,1,0:T(8,128)(2,1)S(1)}, bf16[1,192,2048]{2,1,0:T(8,128)(2,1)}, u32[]{:S(2)}) copy-start(bf16[1,192,2048]{2,1,0:T(8,128)(2,1)} %key_ref.1) | copy-start | bytes 2359300
  49.3 1.1 %copy-start.4 = (bf16[1,192,2048]{2,1,0:T(8,128)(2,1)S(1)}, bf16[1,192,2048]{2,1,0:T(8,128)(2,1)}, u32[]{:S(2)}) copy-start(bf16[1,192,2048]{2,1,0:T(8,128)(2,1)} %value_ref.1) | copy-start | bytes 2359300
  50.4 1.1 %copy-start.5 = (bf16[1,192,2048]{2,1,0:T(8,128)(2,1)S(1)}, bf16[1,192,2048]{2,1,0:T(8,128)(2,1)}, u32[]{:S(2)}) copy-start(bf16[1,192,2048]{2,1,0:T(8,128)(2,1)} %decay_ref.1) | copy-start | bytes 2359300
  67.5 17.6 %copy-start.1 = (bf16[192,2048]{1,0:T(8,128)(2,1)}, bf16[192,2048]{1,0:T(8,128)(2,1)S(1)}, u32[]{:S(2)}) copy-start(bf16[192,2048]{1,0:T(8,128)(2,1)S(1)} %get-tuple-element.6.readout_ref) | copy-start | bytes 2359300
  67.6 17.2 %collective-permute-start = (bf16[16,128,128]{2,1,0:T(8,128)(2,1)S(1)}, bf16[16,128,128]{2,1,0:T(8,128)(2,1)S(1)}, u32[]{:S(2)}, u32[]{:S(2)}) collective-permute-start(bf16[16,128,128]{2,1,0:T(8,128)(2,1)S(1)} %convert_element_type.52), channel_id=1, source_target_pairs={{0,4},{4,8},{8,12},{1,5},{5,9},{9,13},{2,6},{6,10},{10,14},{3,7},{... | collective-permute-start | bytes 1572872 | tf_op jit(solution)/shard_map/ppermute | solution.py:25
  85.1 14.9 %collective-permute-start.1 = (bf16[16,128,128]{2,1,0:T(8,128)(2,1)S(1)}, bf16[16,128,128]{2,1,0:T(8,128)(2,1)S(1)}, u32[]{:S(2)}, u32[]{:S(2)}) collective-permute-start(bf16[16,128,128]{2,1,0:T(8,128)(2,1)S(1)} %fusion.17), channel_id=1, source_target_pairs={{0,4},{4,8},{8,12},{1,5},{5,9},{9,13},{2,6},{6,10},{10,14},{3,7},{... | collective-permute-start | bytes 1572872 | tf_op jit(solution)/shard_map/ppermute | solution.py:25
  100.0 0.8 copy-start.6
Sparse Core Ops, SparseCore 0:
  48.3 21.8 reduce-scatter.1

commit v2 on v1

--- a/solution.py
+++ b/solution.py
@@ -188,6 +188,73 @@
         ).astype(out_ref.dtype)
 
 
+def latent_attention(
+    place_ref,
+    query_ref,
+    even_ref,
+    odd_ref,
+    bias_ref,
+    up_ref,
+    proj_ref,
+    out_ref,
+    total_ref,
+    *,
+    width,
+    score_scale,
+):
+    rows = query_ref.shape[1]
+    lat_dim = up_ref.shape[1]
+    pairs = up_ref.shape[0] // 2
+    wide = even_ref.shape[1]
+    bias = bias_ref[...]
+    bias = jnp.concatenate([bias] * pairs, axis=0) if pairs > 1 else bias
+    contexts = []
+    for key_ref, skip in ((even_ref, 0), (odd_ref, 2 * width - wide)):
+        stacked = [
+            query_ref[0, :, 2 * p * width + skip : 2 * p * width + skip + wide]
+            for p in range(pairs)
+        ]
+        query = jnp.concatenate(stacked, axis=0) if pairs > 1 else stacked[0]
+        scores = lax.dot_general(
+            query, key_ref[...], TRANS, preferred_element_type=jnp.float32
+        )
+        scores = scores * score_scale + bias
+        exponent = jnp.exp(scores - jnp.max(scores, axis=1, keepdims=True))
+        row_total = jnp.sum(exponent, axis=1, keepdims=True)
+        weighted = jnp.dot(
+            exponent.astype(jnp.bfloat16),
+            even_ref[:, :lat_dim],
+            preferred_element_type=jnp.float32,
+        )
+        contexts.append((weighted / row_total).astype(jnp.bfloat16))
+    head_out = []
+    for p in range(pairs):
+        for parity in range(2):
+            head_out.append(
+                jnp.dot(
+                    contexts[parity][p * rows : (p + 1) * rows],
+                    up_ref[2 * p + parity],
+                    preferred_element_type=jnp.float32,
+                ).astype(jnp.bfloat16)
+            )
+    part = jnp.dot(
+        jnp.concatenate(head_out, axis=1), proj_ref[...], preferred_element_type=jnp.float32
+    )
+    step = pl.program_id(0)
+
+    @pl.when(step == 0)
+    def _():
+        total_ref[...] = part
+
+    @pl.when(step > 0)
+    def _():
+        total_ref[...] += part
+
+    @pl.when(step == pl.num_programs(0) - 1)
+    def _():
+        out_ref[...] = total_ref[...].astype(out_ref.dtype)
+
+
 def local(
     kda_query,
     kda_key,
@@ -258,14 +325,81 @@
         carried[:, None],
     )
 
-    inbound_state = None
-    for hop in range(hops):
+    width = latents.shape[2]
+    vhead = value_up.shape[2]
+    model = out_proj.shape[1]
+    row_count = block_rows.shape[0]
+    key_pos = first_pos - hops * tokens_dev + jnp.arange(row_count, dtype=jnp.int32)
+    key_doc = doc_index(key_pos, doc_ends)
+    allowed = (
+        (key_pos[None, :] <= positions[:, None])
+        & (key_pos[None, :] >= 0)
+        & (key_doc[None, :] == doc_ids[:, None])
+    )
+    bias = jnp.where(allowed, 0.0, masked_score)
+    spare = -width % 128
+    even_rows = jnp.pad(block_rows, ((0, 0), (0, spare)))
+    odd_rows = jnp.pad(block_rows, ((0, 0), (spare, 0)))
+    rows = tokens_dev // 2
+
+    def attention(place, dtype):
+        keys = pl.BlockSpec((row_count, width + spare), lambda i, at: (0, 0))
+        return pl.pallas_call(
+            functools.partial(
+                latent_attention, width=width, score_scale=1.0 / math.sqrt(NOPE + ROPE)
+            ),
+            grid_spec=pltpu.PrefetchScalarGridSpec(
+                num_scalar_prefetch=1,
+                grid=(steps,),
+                in_specs=[
+                    pl.BlockSpec((1, rows, HEADS_STEP * width), lambda i, at: (0, at[0], i)),
+                    keys,
+                    keys,
+                    pl.BlockSpec((rows, row_count), lambda i, at: (at[0], 0)),
+                    pl.BlockSpec((HEADS_STEP,) + value_up.shape[1:], lambda i, at: (i, 0, 0)),
+                    pl.BlockSpec((HEADS_STEP * vhead, model), lambda i, at: (i, 0)),
+                ],
+                out_specs=pl.BlockSpec((rows, model), lambda i, at: (0, 0)),
+                scratch_shapes=[pltpu.VMEM((rows, model), jnp.float32)],
+            ),
+            out_shape=jax.ShapeDtypeStruct((rows, model), dtype),
+            compiler_params=pltpu.CompilerParams(vmem_limit_bytes=48 << 20),
+            cost_estimate=pl.CostEstimate(
+                flops=12_000_000_000, bytes_accessed=16_000_000, transcendentals=0
+            ),
+        )(place, mla_query, even_rows, odd_rows, bias, value_up, out_proj)
+
+    def relayed(inbound_state, hop):
         outgoing = offset
         if hop > 0:
             outgoing = offset + jnp.einsum(
                 "hcd,hdv->hcv", transition, inbound_state, preferred_element_type=jnp.float32
             )
-        inbound_state = from_behind(outgoing.astype(jnp.bfloat16), "ctx", 1)
+        return outgoing.astype(jnp.bfloat16)
+
+    head_count = lax.axis_size("head")
+    mine = lax.axis_index("head") if head_count == 2 else jnp.int32(1)
+    first, outgoing = lax.optimization_barrier(((1 - mine)[None], relayed(None, 0)))
+    inbound_state = from_behind(outgoing, "ctx", 1)
+    far_part = attention(first, jnp.bfloat16)
+    if head_count == 2:
+        far_part = lax.ppermute(far_part, "head", [(0, 1), (1, 0)])
+    second = mine[None]
+    for hop in range(1, hops):
+        outgoing = relayed(inbound_state, hop)
+        second, outgoing = lax.optimization_barrier((second, outgoing))
+        inbound_state = from_behind(outgoing, "ctx", 1)
+    if head_count == 2:
+        near_part = attention(second, jnp.float32)
+        mixed = (near_part + far_part.astype(jnp.float32)).astype(jnp.bfloat16)
+    else:
+        near_part = attention(second, jnp.bfloat16)
+        mixed = lax.psum_scatter(
+            jnp.concatenate([far_part, near_part], axis=0),
+            "head",
+            scatter_dimension=0,
+            tiled=True,
+        )
     kda_out = pl.pallas_call(
         delta_readout,
         grid=(steps,),
@@ -276,49 +410,6 @@
             flops=100_000_000, bytes_accessed=4_000_000, transcendentals=0
         ),
     )(readout, local_part, inbound_state)
-
-    width = latents.shape[2]
-    lat_dim = value_up.shape[1]
-    score_scale = 1.0 / math.sqrt(NOPE + ROPE)
-    query_flat = mla_query[0].reshape(tokens_dev * heads_dev, width)
-    row_pos = jnp.repeat(positions, heads_dev)
-    row_doc = jnp.repeat(doc_ids, heads_dev)
-    row_total_count = tokens_dev * heads_dev
-    row_peak = jnp.full((row_total_count,), masked_score, jnp.float32)
-    row_count = block_rows.shape[0]
-    key_pos = first_pos - hops * tokens_dev + jnp.arange(row_count, dtype=jnp.int32)
-    key_doc = doc_index(key_pos, doc_ends)
-    scores = (
-        lax.dot_general(
-            query_flat, block_rows, (((1,), (1,)), ((), ())), preferred_element_type=jnp.float32
-        )
-        * score_scale
-    )
-    allowed = (
-        (key_pos[None, :] <= row_pos[:, None])
-        & (key_pos[None, :] >= 0)
-        & (key_doc[None, :] == row_doc[:, None])
-    )
-    new_peak = jnp.maximum(row_peak, jnp.max(jnp.where(allowed, scores, masked_score), axis=1))
-    exponent = jnp.where(allowed, jnp.exp(scores - new_peak[:, None]), 0.0)
-    row_total = jnp.sum(exponent, axis=1)
-    weighted = jnp.dot(
-        exponent.astype(jnp.bfloat16), block_rows[:, :lat_dim], preferred_element_type=jnp.float32
-    )
-    row_peak, row_total, weighted = (new_peak, row_total, weighted)
-    context = (
-        (weighted / row_total[:, None]).astype(jnp.bfloat16).reshape(tokens_dev, heads_dev, lat_dim)
-    )
-    head_out = jnp.einsum(
-        "thl,hlv->thv", context, value_up, preferred_element_type=jnp.float32
-    ).astype(jnp.bfloat16)
-    head_out = head_out.reshape(tokens_dev, heads_dev * value_up.shape[2])
-    mixed = lax.psum_scatter(
-        jnp.dot(head_out, out_proj, preferred_element_type=jnp.float32).astype(jnp.bfloat16),
-        "head",
-        scatter_dimension=0,
-        tiled=True,
-    )
     return (kda_out, mixed[None])
 
 

time: 113 us -> 71.7 us (0.63)
  waiting for transfers between devices: 21.8 us -> 0.01 us
  Pallas kernels: 20 us -> 41.7 us
  matrix products: 17.6 us -> 0.31 us
  between operations: 14.3 us -> 0.81 us
  starting transfers between devices: 19.9 us -> 15.1 us
  local copies, waits for them, and re-layouts: 11.9 us -> 8.85 us
  other arithmetic: 6.2 us -> 4.45 us
    ppermute x4, waiting for transfers between devices: 21.8 us -> 0.01 us  [from_behind(): return lax.ppermute(value, axis, pairs)]
    pallas_call x0 -> x2, Pallas kernels: none -> 21.7 us  [attention(): pl.pallas_call(functools.partial(latent_attention, width=width, score_sca...]
    dot_general x5 -> x1, matrix products: 17.6 us -> 0.31 us  [relayed(): jnp.einsum('hcd,hdv->hcv', transition, inbound_state, preferred_element_t...]
    another operation x1 -> x0, local copies, waits for them, and re-layouts: 6.97 us -> none  [local(): query_flat = mla_query[0].reshape(tokens_dev * heads_dev, width)]
    ppermute x4, starting transfers between devices: 19.9 us -> 13.5 us  [from_behind(): return lax.ppermute(value, axis, pairs)]
    reduce_sum x1 -> x0, other arithmetic: 3.8 us -> none  [local(): row_total = jnp.sum(exponent, axis=1)]
    unnamed x24 -> x16, local copies, waits for them, and re-layouts: 4.24 us -> 7.38 us
    ppermute x0 -> x1, starting transfers between devices: none -> 1.56 us  [local(): far_part = lax.ppermute(far_part, 'head', [(0, 1), (1, 0)])]
  transfers between devices with their start and end apart: 5 -> 5, of which waited for: 2 -> 0; matrix products, arithmetic and copies ran while one was open for 9% -> 9% of each run, Pallas kernels for 18% -> 53%
where the time goes in v2:
time: 71.7 us; the launch traced here: 71.2 us
  Pallas kernels  41.7 us (58%)
  starting transfers between devices  15.1 us (21%)
  local copies, waits for them, and re-layouts  8.85 us (12%)
  other arithmetic  4.45 us (6%)
  between operations  0.81 us (1%)
    pallas_call x2, Pallas kernels, attention(): pl.pallas_call(functools.partial(latent_attention, width=width, score_sca...  21.7 us
    pallas_call x1, Pallas kernels, local(): pl.pallas_call(delta_terms, grid=(steps,), in_specs=[packed] * 4 + [pl.Bl...  15.9 us
    ppermute x4, starting transfers between devices, from_behind(): return lax.ppermute(value, axis, pairs)  13.5 us
    unnamed x16, local copies, waits for them, and re-layouts  7.38 us
    pallas_call x1, Pallas kernels, local(): pl.pallas_call(delta_readout, grid=(steps,), in_specs=[flat, flat, square...  4.02 us
    ppermute x1, starting transfers between devices, local(): far_part = lax.ppermute(far_part, 'head', [(0, 1), (1, 0)])  1.56 us
  transfers between devices with their start and end apart: 5, of which 0 were waited for; matrix products, arithmetic and copies ran while one was open for 9% of the time, Pallas kernels for 53%

profile of v2, /device:TPU:0, one launch (start us, length us, event | category | flops | bytes accessed | tf_op | source)
XLA Modules:
  0.0 71.2 jit_solution(786174681270544166)
XLA Ops:
  0.6 4.9 %collective-permute-start.3 = (bf16[192,576]{1,0:T(8,128)(2,1)}, bf16[192,576]{1,0:T(8,128)(2,1)S(1)}, u32[]{:S(2)}, u32[]{:S(2)}) collective-permute-start(bf16[192,576]{1,0:T(8,128)(2,1)} %bitcast.15), channel_id=1, source_target_pairs={{0,4},{4,8},{8,12},{1,5},{5,9},{9,13},{2,6},{6,10},{10,14},{3,7},{... | collective-permute-start | bytes 663560 | tf_op jit(solution)/shard_map/ppermute | solution.py:25
  5.6 5.2 %collective-permute-start.2 = (bf16[192,576]{1,0:T(8,128)(2,1)}, bf16[192,576]{1,0:T(8,128)(2,1)}, u32[]{:S(2)}, u32[]{:S(2)}) collective-permute-start(bf16[192,576]{1,0:T(8,128)(2,1)} %bitcast.16), channel_id=1, source_target_pairs={{0,8},{4,12},{1,9},{5,13},{2,10},{6,14},{3,11},{7,15},{16,24},{20,... | collective-permute-start | bytes 663560 | tf_op jit(solution)/shard_map/ppermute | solution.py:25
  10.8 0.7 %reshape_squeeze.3 = f32[4,4,192]{2,1,0:T(4,128)S(1)} reshape(f32[1,16,192]{2,1,0:T(8,128)} %param.14) | data formatting | bytes 24576 | tf_op jit(solution)/shard_map/reshape;squeeze | solution.py:290
  11.5 0.2 copy.18
  11.7 0.8 %reduce-window.4 = s32[8,1]{0,1:T(1,128)S(1)} reduce-window(s32[8,1]{0,1:T(1,128)} %bitcast.20, s32[]{:T(128)} %constant.10.clone.1), window={size=8x1 pad=7_0x0_0}, to_apply=%region_0.0 | reduce-window | flops 56 | bytes 68 | tf_op jit(solution)/shard_map/reduce-window
  12.5 0.1 convert_reduce_fusion.1
  12.6 0.1 copy.21.doc_col_ref
  12.8 0.6 fusion.2
  13.4 0.7 compare_convert_fusion.carried_ref
  14.1 0.0 copy-start.2
  14.1 1.1 %copy-done.2 = bf16[1,192,2048]{2,1,0:T(8,128)(2,1)S(1)} copy-done((bf16[1,192,2048]{2,1,0:T(8,128)(2,1)S(1)}, bf16[1,192,2048]{2,1,0:T(8,128)(2,1)}, u32[]{:S(2)}) %copy-start.2) | copy-done | bytes 786456
  15.2 0.0 copy-start.3
  15.2 1.1 %copy-done.3 = bf16[1,192,2048]{2,1,0:T(8,128)(2,1)S(1)} copy-done((bf16[1,192,2048]{2,1,0:T(8,128)(2,1)S(1)}, bf16[1,192,2048]{2,1,0:T(8,128)(2,1)}, u32[]{:S(2)}) %copy-start.3) | copy-done | bytes 786456
  16.3 0.0 copy-start.4
  16.3 1.1 %copy-done.4 = bf16[1,192,2048]{2,1,0:T(8,128)(2,1)S(1)} copy-done((bf16[1,192,2048]{2,1,0:T(8,128)(2,1)S(1)}, bf16[1,192,2048]{2,1,0:T(8,128)(2,1)}, u32[]{:S(2)}) %copy-start.4) | copy-done | bytes 786456
  17.5 0.0 copy-start.5
  17.5 1.1 %copy-done.5 = bf16[1,192,2048]{2,1,0:T(8,128)(2,1)S(1)} copy-done((bf16[1,192,2048]{2,1,0:T(8,128)(2,1)S(1)}, bf16[1,192,2048]{2,1,0:T(8,128)(2,1)}, u32[]{:S(2)}) %copy-start.5) | copy-done | bytes 786456
  18.6 15.9 %shard_map.113 = (bf16[192,2048]{1,0:T(8,128)(2,1)S(1)}, f32[192,2048]{1,0:T(8,128)}, bf16[16,128,128]{2,1,0:T(8,128)(2,1)S(1)}, f32[16,128,128]{2,1,0:T(8,128)S(1)}) custom-call(bf16[1,192,2048]{2,1,0:T(8,128)(2,1)S(1)} %copy-done.2, bf16[1,192,2048]{2,1,0:T(8,128)(2,1)S(1)} %copy-done.3, bf16[1,192,2048]{2,1,0:T(8,128)(2,1)S(1)} %copy-done.4, ...), custom_call_target="tpu_custom_call" | custom-call | flops 20000000000 | bytes 8000000 | tf_op jit(solution)/shard_map/pallas_call | solution.py:296
  34.5 0.0 copy-start
  34.5 0.9 %copy-done = bf16[192,2048]{1,0:T(8,128)(2,1)} copy-done((bf16[192,2048]{1,0:T(8,128)(2,1)}, bf16[192,2048]{1,0:T(8,128)(2,1)S(1)}, u32[]{:S(2)}) %copy-start) | copy-done | bytes 786456
  35.4 0.0 copy-start.7
  35.4 0.1 convert_element_type.47
  35.5 1.5 %collective-permute-start = (bf16[16,128,128]{2,1,0:T(8,128)(2,1)S(1)}, bf16[16,128,128]{2,1,0:T(8,128)(2,1)S(1)}, u32[]{:S(2)}, u32[]{:S(2)}) collective-permute-start(bf16[16,128,128]{2,1,0:T(8,128)(2,1)S(1)} %convert_element_type.47), channel_id=1, source_target_pairs={{0,4},{4,8},{8,12},{1,5},{5,9},{9,13},{2,6},{6,10},{10,14},{3,7},{... | collective-permute-start | bytes 1572872 | tf_op jit(solution)/shard_map/ppermute | solution.py:25
  37.0 0.1 convert_reduce_fusion
  37.1 0.2 and_select_fusion.bias_ref
  37.3 0.0 collective-permute-done.3
  37.3 0.0 collective-permute-done.2
  37.3 0.0 copy-done.7
  37.3 1.0 %pad_maximum_fusion = bf16[576,576]{1,0:T(8,128)(2,1)S(1)} fusion(bf16[192,576]{1,0:T(8,128)(2,1)S(1)} %bitcast.17, bf16[192,576]{1,0:T(8,128)(2,1)S(1)} %collective-permute-done.3, bf16[192,576]{1,0:T(8,128)(2,1)} %collective-permute-done.2), kind=kLoop, calls=%fused_computation.3 | loop fusion | flops 1990656 | bytes 1327104 | tf_op jit(solution)/shard_map/concatenate | solution.py:285
  38.3 0.0 copy-start.1
  38.4 0.4 fusion.3
  38.8 1.1 %copy-done.1 = bf16[16,512,128]{2,1,0:T(8,128)(2,1)S(1)} copy-done((bf16[16,512,128]{2,1,0:T(8,128)(2,1)S(1)}, bf16[16,512,128]{2,1,0:T(8,128)(2,1)}, u32[]{:S(2)}) %copy-start.1) | copy-done | bytes 2097176
  39.9 10.8 %shard_map.116 = bf16[96,2304]{1,0:T(8,128)(2,1)S(1)} custom-call(s32[1]{0:T(128)} %bitcast.6.place_ref, bf16[1,192,9216]{2,1,0:T(8,128)(2,1)} %query_ref.5, bf16[576,640]{1,0:T(8,128)(2,1)S(1)} %get-tuple-element.19.even_ref, bf16[576,640]{1,0:T(8,128)(2,1)S(1)} %get-tuple-element.18.odd_ref, f32[192,576]{1,0:T(8,128)S(1)} %and_select_fusion.bias_ref, ...), custom_call_target="tpu_custom_call" | custom-call | flops 12000000000 | bytes 16000000 | tf_op jit(solution)/shard_map/pallas_call | solution.py:347
  50.8 1.6 %collective-permute-start.4 = (bf16[96,2304]{1,0:T(8,128)(2,1)S(1)}, bf16[96,2304]{1,0:T(8,128)(2,1)S(1)}, u32[]{:S(2)}, u32[]{:S(2)}) collective-permute-start(bf16[96,2304]{1,0:T(8,128)(2,1)S(1)} %shard_map.116), channel_id=1, source_target_pairs={{0,2},{2,0},{1,3},{3,1},{4,6},{6,4},{5,7},{7,5},{8,10},{10,8},{9,1... | collective-permute-start | bytes 1327112 | tf_op jit(solution)/shard_map/ppermute | solution.py:386
  52.3 0.0 collective-permute-done
  52.4 0.3 fusion
  52.7 1.9 %collective-permute-start.1 = (bf16[16,128,128]{2,1,0:T(8,128)(2,1)S(1)}, bf16[16,128,128]{2,1,0:T(8,128)(2,1)S(1)}, u32[]{:S(2)}, u32[]{:S(2)}) collective-permute-start(bf16[16,128,128]{2,1,0:T(8,128)(2,1)S(1)} %fusion), channel_id=1, source_target_pairs={{0,4},{4,8},{8,12},{1,5},{5,9},{9,13},{2,6},{6,10},{10,14},{3,7},{... | collective-permute-start | bytes 1572872 | tf_op jit(solution)/shard_map/ppermute | solution.py:25
  54.6 10.9 %shard_map.115 = f32[96,2304]{1,0:T(8,128)S(1)} custom-call(s32[1]{0:T(128)} %bitcast.5.place_ref, bf16[1,192,9216]{2,1,0:T(8,128)(2,1)} %query_ref.5, bf16[576,640]{1,0:T(8,128)(2,1)S(1)} %get-tuple-element.19.even_ref, bf16[576,640]{1,0:T(8,128)(2,1)S(1)} %get-tuple-element.18.odd_ref, f32[192,576]{1,0:T(8,128)S(1)} %and_select_fusion.bias_ref, ...), custom_call_target="tpu_custom_call" | custom-call | flops 12000000000 | bytes 16000000 | tf_op jit(solution)/shard_map/pallas_call | solution.py:347
  65.5 0.0 collective-permute-done.4
  65.5 0.8 %fusion.1 = bf16[1,96,2304]{2,1,0:T(8,128)(2,1)} fusion(f32[96,2304]{1,0:T(8,128)S(1)} %shard_map.115, bf16[96,2304]{1,0:T(8,128)(2,1)S(1)} %collective-permute-done.4), kind=kLoop, calls=%fused_computation.5 | loop fusion | flops 663552 | bytes 1769472 | tf_op jit(solution)/shard_map/broadcast_in_dim | solution.py:413
  66.3 0.0 collective-permute-done.1.state_ref
  66.3 0.0 copy-start.6
  66.3 0.8 %copy-done.6 = bf16[16,128,128]{2,1,0:T(8,128)(2,1)} copy-done((bf16[16,128,128]{2,1,0:T(8,128)(2,1)}, bf16[16,128,128]{2,1,0:T(8,128)(2,1)S(1)}, u32[]{:S(2)}) %copy-start.6) | copy-done | bytes 524312
  67.1 4.0 %shard_map.114 = bf16[1,192,2048]{2,1,0:T(8,128)(2,1)} custom-call(bf16[192,2048]{1,0:T(8,128)(2,1)} %copy-done, f32[192,2048]{1,0:T(8,128)} %get-tuple-element.11.local_ref, bf16[16,128,128]{2,1,0:T(8,128)(2,1)} %copy-done.6), custom_call_target="tpu_custom_call" | custom-call | flops 100000000 | bytes 4000000 | tf_op jit(solution)/shard_map/pallas_call | solution.py:403
  (3 shorter events, 0.0 us)
Async XLA Ops:
  0.6 36.7 %collective-permute-start.3 = (bf16[192,576]{1,0:T(8,128)(2,1)}, bf16[192,576]{1,0:T(8,128)(2,1)S(1)}, u32[]{:S(2)}, u32[]{:S(2)}) collective-permute-start(bf16[192,576]{1,0:T(8,128)(2,1)} %bitcast.15), channel_id=1, source_target_pairs={{0,4},{4,8},{8,12},{1,5},{5,9},{9,13},{2,6},{6,10},{10,14},{3,7},{... | collective-permute-start | bytes 663560 | tf_op jit(solution)/shard_map/ppermute | solution.py:25
  5.6 31.7 %collective-permute-start.2 = (bf16[192,576]{1,0:T(8,128)(2,1)}, bf16[192,576]{1,0:T(8,128)(2,1)}, u32[]{:S(2)}, u32[]{:S(2)}) collective-permute-start(bf16[192,576]{1,0:T(8,128)(2,1)} %bitcast.16), channel_id=1, source_target_pairs={{0,8},{4,12},{1,9},{5,13},{2,10},{6,14},{3,11},{7,15},{16,24},{20,... | collective-permute-start | bytes 663560 | tf_op jit(solution)/shard_map/ppermute | solution.py:25
  14.1 1.1 %copy-start.2 = (bf16[1,192,2048]{2,1,0:T(8,128)(2,1)S(1)}, bf16[1,192,2048]{2,1,0:T(8,128)(2,1)}, u32[]{:S(2)}) copy-start(bf16[1,192,2048]{2,1,0:T(8,128)(2,1)} %query_ref.3) | copy-start | bytes 2359300
  15.2 1.1 %copy-start.3 = (bf16[1,192,2048]{2,1,0:T(8,128)(2,1)S(1)}, bf16[1,192,2048]{2,1,0:T(8,128)(2,1)}, u32[]{:S(2)}) copy-start(bf16[1,192,2048]{2,1,0:T(8,128)(2,1)} %key_ref.1) | copy-start | bytes 2359300
  16.3 1.1 %copy-start.4 = (bf16[1,192,2048]{2,1,0:T(8,128)(2,1)S(1)}, bf16[1,192,2048]{2,1,0:T(8,128)(2,1)}, u32[]{:S(2)}) copy-start(bf16[1,192,2048]{2,1,0:T(8,128)(2,1)} %value_ref.1) | copy-start | bytes 2359300
  17.5 1.1 %copy-start.5 = (bf16[1,192,2048]{2,1,0:T(8,128)(2,1)S(1)}, bf16[1,192,2048]{2,1,0:T(8,128)(2,1)}, u32[]{:S(2)}) copy-start(bf16[1,192,2048]{2,1,0:T(8,128)(2,1)} %decay_ref.1) | copy-start | bytes 2359300
  34.5 0.9 %copy-start = (bf16[192,2048]{1,0:T(8,128)(2,1)}, bf16[192,2048]{1,0:T(8,128)(2,1)S(1)}, u32[]{:S(2)}) copy-start(bf16[192,2048]{1,0:T(8,128)(2,1)S(1)} %get-tuple-element.10.readout_ref) | copy-start | bytes 2359300
  35.4 1.9 %copy-start.7 = (bf16[1,192,576]{2,1,0:T(8,128)(2,1)S(1)}, bf16[1,192,576]{2,1,0:T(8,128)(2,1)}, u32[]{:S(2)}) copy-start(bf16[1,192,576]{2,1,0:T(8,128)(2,1)} %param.16) | copy-start | bytes 663556
  35.5 16.8 %collective-permute-start = (bf16[16,128,128]{2,1,0:T(8,128)(2,1)S(1)}, bf16[16,128,128]{2,1,0:T(8,128)(2,1)S(1)}, u32[]{:S(2)}, u32[]{:S(2)}) collective-permute-start(bf16[16,128,128]{2,1,0:T(8,128)(2,1)S(1)} %convert_element_type.47), channel_id=1, source_target_pairs={{0,4},{4,8},{8,12},{1,5},{5,9},{9,13},{2,6},{6,10},{10,14},{3,7},{... | collective-permute-start | bytes 1572872 | tf_op jit(solution)/shard_map/ppermute | solution.py:25
  38.3 1.6 %copy-start.1 = (bf16[16,512,128]{2,1,0:T(8,128)(2,1)S(1)}, bf16[16,512,128]{2,1,0:T(8,128)(2,1)}, u32[]{:S(2)}) copy-start(bf16[16,512,128]{2,1,0:T(8,128)(2,1)} %up_ref.3) | copy-start | bytes 6291460
  50.8 14.7 %collective-permute-start.4 = (bf16[96,2304]{1,0:T(8,128)(2,1)S(1)}, bf16[96,2304]{1,0:T(8,128)(2,1)S(1)}, u32[]{:S(2)}, u32[]{:S(2)}) collective-permute-start(bf16[96,2304]{1,0:T(8,128)(2,1)S(1)} %shard_map.116), channel_id=1, source_target_pairs={{0,2},{2,0},{1,3},{3,1},{4,6},{6,4},{5,7},{7,5},{8,10},{10,8},{9,1... | collective-permute-start | bytes 1327112 | tf_op jit(solution)/shard_map/ppermute | solution.py:386
  52.7 13.7 %collective-permute-start.1 = (bf16[16,128,128]{2,1,0:T(8,128)(2,1)S(1)}, bf16[16,128,128]{2,1,0:T(8,128)(2,1)S(1)}, u32[]{:S(2)}, u32[]{:S(2)}) collective-permute-start(bf16[16,128,128]{2,1,0:T(8,128)(2,1)S(1)} %fusion), channel_id=1, source_target_pairs={{0,4},{4,8},{8,12},{1,5},{5,9},{9,13},{2,6},{6,10},{10,14},{3,7},{... | collective-permute-start | bytes 1572872 | tf_op jit(solution)/shard_map/ppermute | solution.py:25
  66.3 0.8 %copy-start.6 = (bf16[16,128,128]{2,1,0:T(8,128)(2,1)}, bf16[16,128,128]{2,1,0:T(8,128)(2,1)S(1)}, u32[]{:S(2)}) copy-start(bf16[16,128,128]{2,1,0:T(8,128)(2,1)S(1)} %collective-permute-done.1.state_ref) | copy-start | bytes 1572868

commit v3 on v2

--- a/solution.py
+++ b/solution.py
@@ -23,6 +23,10 @@
     peers = lax.axis_size(axis)
     pairs = [(i, i + by) for i in range(peers) if 0 <= i + by < peers]
     return lax.ppermute(value, axis, pairs)
+
+
+def in_place(value):
+    return pltpu.with_memory_space_constraint(value, pltpu.HBM)
 
 
 def doc_index(position_list, doc_ends):
@@ -157,22 +161,17 @@
     for h in heads:
         lanes = slice(h * state_dim, (h + 1) * state_dim)
         whole = jnp.concatenate(solved[h], axis=0)
-        whole_halves = halves(whole)
         for a in range(spans):
             here = slice(a * SPAN, (a + 1) * SPAN)
             seen = (a + 1) * SPAN
-            attend_high, attend_low = halves(attends[h][a])
-            read = (
-                dot_once(attend_high, whole_halves[1][:seen], ROWS)
-                + dot_once(attend_low, whole_halves[0][:seen], ROWS)
-            ) + dot_once(attend_high, whole_halves[0][:seen], ROWS)
+            read = dot_once(attends[h][a], whole[:seen], ROWS)
             readout_ref[here, lanes] = (
                 carried[here] * queries[h][here] * growths[h][here] - read[:, :state_dim]
             ).astype(readout_ref.dtype)
             local_ref[here, lanes] = read[:, state_dim:]
         last = summed[h][tokens - 1 : tokens]
         key_decay = keys[h] * jnp.exp(last - summed[h]) * tail
-        moved = dot_split(key_decay, whole, OVER)
+        moved = dot_once(key_decay, whole, OVER)
         kept = carried[tokens - 1 : tokens] * growths[h][tokens - 1 : tokens]
         transition_ref[h] = (eye * kept - moved[:, :state_dim]).astype(transition_ref.dtype)
         offset_ref[h] = moved[:, state_dim:]
@@ -200,13 +199,16 @@
     total_ref,
     *,
     width,
+    first_key,
     score_scale,
 ):
     rows = query_ref.shape[1]
+    key_count = bias_ref.shape[2]
+    keys = pl.ds(pl.multiple_of(place_ref[0] * rows + first_key, math.gcd(rows, 16)), key_count)
     lat_dim = up_ref.shape[1]
     pairs = up_ref.shape[0] // 2
     wide = even_ref.shape[1]
-    bias = bias_ref[...]
+    bias = bias_ref[0]
     bias = jnp.concatenate([bias] * pairs, axis=0) if pairs > 1 else bias
     contexts = []
     for key_ref, skip in ((even_ref, 0), (odd_ref, 2 * width - wide)):
@@ -216,14 +218,14 @@
         ]
         query = jnp.concatenate(stacked, axis=0) if pairs > 1 else stacked[0]
         scores = lax.dot_general(
-            query, key_ref[...], TRANS, preferred_element_type=jnp.float32
+            query, key_ref[keys, :], TRANS, preferred_element_type=jnp.float32
         )
         scores = scores * score_scale + bias
         exponent = jnp.exp(scores - jnp.max(scores, axis=1, keepdims=True))
         row_total = jnp.sum(exponent, axis=1, keepdims=True)
         weighted = jnp.dot(
             exponent.astype(jnp.bfloat16),
-            even_ref[:, :lat_dim],
+            even_ref[keys, :lat_dim],
             preferred_element_type=jnp.float32,
         )
         contexts.append((weighted / row_total).astype(jnp.bfloat16))
@@ -315,10 +317,10 @@
             flops=20_000_000_000, bytes_accessed=8_000_000, transcendentals=0
         ),
     )(
-        kda_query,
-        kda_key,
-        kda_value,
-        log_decay,
+        in_place(kda_query),
+        in_place(kda_key),
+        in_place(kda_value),
+        in_place(log_decay),
         strength,
         doc_ids[:, None],
         doc_ids[None, :],
@@ -329,24 +331,30 @@
     vhead = value_up.shape[2]
     model = out_proj.shape[1]
     row_count = block_rows.shape[0]
-    key_pos = first_pos - hops * tokens_dev + jnp.arange(row_count, dtype=jnp.int32)
-    key_doc = doc_index(key_pos, doc_ends)
+    rows = tokens_dev // 2
+    back = -(-(longest - 1) // rows) * rows
+    first_key = hops * tokens_dev - back
+    half_pos = positions.reshape(2, rows)
+    key_pos = half_pos[:, :1] - back + jnp.arange(back + rows, dtype=jnp.int32)[None, :]
+    key_doc = doc_index(key_pos.reshape(-1), doc_ends).reshape(key_pos.shape)
     allowed = (
-        (key_pos[None, :] <= positions[:, None])
-        & (key_pos[None, :] >= 0)
-        & (key_doc[None, :] == doc_ids[:, None])
+        (key_pos[:, None, :] <= half_pos[:, :, None])
+        & (key_pos[:, None, :] >= 0)
+        & (key_doc[:, None, :] == doc_ids.reshape(2, rows)[:, :, None])
     )
     bias = jnp.where(allowed, 0.0, masked_score)
     spare = -width % 128
     even_rows = jnp.pad(block_rows, ((0, 0), (0, spare)))
     odd_rows = jnp.pad(block_rows, ((0, 0), (spare, 0)))
-    rows = tokens_dev // 2
 
     def attention(place, dtype):
         keys = pl.BlockSpec((row_count, width + spare), lambda i, at: (0, 0))
         return pl.pallas_call(
             functools.partial(
-                latent_attention, width=width, score_scale=1.0 / math.sqrt(NOPE + ROPE)
+                latent_attention,
+                width=width,
+                first_key=first_key,
+                score_scale=1.0 / math.sqrt(NOPE + ROPE),
             ),
             grid_spec=pltpu.PrefetchScalarGridSpec(
                 num_scalar_prefetch=1,
@@ -355,7 +363,7 @@
                     pl.BlockSpec((1, rows, HEADS_STEP * width), lambda i, at: (0, at[0], i)),
                     keys,
                     keys,
-                    pl.BlockSpec((rows, row_count), lambda i, at: (at[0], 0)),
+                    pl.BlockSpec((1, rows, back + rows), lambda i, at: (at[0], 0, 0)),
                     pl.BlockSpec((HEADS_STEP,) + value_up.shape[1:], lambda i, at: (i, 0, 0)),
                     pl.BlockSpec((HEADS_STEP * vhead, model), lambda i, at: (i, 0)),
                 ],
@@ -367,7 +375,7 @@
             cost_estimate=pl.CostEstimate(
                 flops=12_000_000_000, bytes_accessed=16_000_000, transcendentals=0
             ),
-        )(place, mla_query, even_rows, odd_rows, bias, value_up, out_proj)
+        )(place, in_place(mla_query), even_rows, odd_rows, bias, in_place(value_up), in_place(out_proj))
 
     def relayed(inbound_state, hop):
         outgoing = offset

time: 71.7 us -> 63.9 us (0.89)
  local copies, waits for them, and re-layouts: 8.85 us -> 4.41 us
  Pallas kernels: 41.7 us -> 38.1 us
    unnamed x16 -> x8, local copies, waits for them, and re-layouts: 7.38 us -> 2.84 us
    pallas_call x2, Pallas kernels: 21.7 us -> 19.3 us  [attention(): pl.pallas_call(functools.partial(latent_attention, width=width, first_key...]
    pallas_call x1, Pallas kernels: 15.9 us -> 14.8 us  [local(): pl.pallas_call(delta_terms, grid=(steps,), in_specs=[packed] * 4 + [pl.Bl...]
  transfers between devices with their start and end apart: 5 -> 5, of which waited for: 0 -> 0; matrix products, arithmetic and copies ran while one was open for 9% -> 10% of each run, Pallas kernels for 53% -> 54%
where the time goes in v3:
time: 63.9 us; the launch traced here: 63.4 us
  Pallas kernels  38.1 us (60%)
  starting transfers between devices  15.1 us (24%)
  other arithmetic  4.66 us (7%)
  local copies, waits for them, and re-layouts  4.41 us (7%)
  between operations  0.81 us (1%)
    pallas_call x2, Pallas kernels, attention(): pl.pallas_call(functools.partial(latent_attention, width=width, first_key...  19.3 us
    pallas_call x1, Pallas kernels, local(): pl.pallas_call(delta_terms, grid=(steps,), in_specs=[packed] * 4 + [pl.Bl...  14.8 us
    ppermute x4, starting transfers between devices, from_behind(): return lax.ppermute(value, axis, pairs)  13.6 us
    pallas_call x1, Pallas kernels, local(): pl.pallas_call(delta_readout, grid=(steps,), in_specs=[flat, flat, square...  4.02 us
    unnamed x8, local copies, waits for them, and re-layouts  2.84 us
    ppermute x1, starting transfers between devices, local(): far_part = lax.ppermute(far_part, 'head', [(0, 1), (1, 0)])  1.56 us
  transfers between devices with their start and end apart: 5, of which 0 were waited for; matrix products, arithmetic and copies ran while one was open for 10% of the time, Pallas kernels for 54%

profile of v3, /device:TPU:0, one launch (start us, length us, event | category | flops | bytes accessed | tf_op | source)
XLA Modules:
  0.0 63.4 jit_solution(5434067954928185939)
XLA Ops:
  0.6 4.9 %collective-permute-start.3 = (bf16[192,576]{1,0:T(8,128)(2,1)}, bf16[192,576]{1,0:T(8,128)(2,1)S(1)}, u32[]{:S(2)}, u32[]{:S(2)}) collective-permute-start(bf16[192,576]{1,0:T(8,128)(2,1)} %bitcast.15), channel_id=1, source_target_pairs={{0,4},{4,8},{8,12},{1,5},{5,9},{9,13},{2,6},{6,10},{10,14},{3,7},{... | collective-permute-start | bytes 663560 | tf_op jit(solution)/shard_map/ppermute | solution.py:25
  5.6 5.2 %collective-permute-start.2 = (bf16[192,576]{1,0:T(8,128)(2,1)}, bf16[192,576]{1,0:T(8,128)(2,1)}, u32[]{:S(2)}, u32[]{:S(2)}) collective-permute-start(bf16[192,576]{1,0:T(8,128)(2,1)} %bitcast.16), channel_id=1, source_target_pairs={{0,8},{4,12},{1,9},{5,13},{2,10},{6,14},{3,11},{7,15},{16,24},{20,... | collective-permute-start | bytes 663560 | tf_op jit(solution)/shard_map/ppermute | solution.py:25
  10.8 0.7 %reshape_squeeze.3 = f32[4,4,192]{2,1,0:T(4,128)S(1)} reshape(f32[1,16,192]{2,1,0:T(8,128)} %param.14) | data formatting | bytes 24576 | tf_op jit(solution)/shard_map/reshape;squeeze | solution.py:292
  11.5 0.2 copy.25
  11.7 0.8 %reduce-window.4 = s32[8,1]{0,1:T(1,128)S(1)} reduce-window(s32[8,1]{0,1:T(1,128)} %bitcast.20, s32[]{:T(128)} %constant.23.clone.1), window={size=8x1 pad=7_0x0_0}, to_apply=%region_0.0 | reduce-window | flops 56 | bytes 68 | tf_op jit(solution)/shard_map/reduce-window
  12.5 0.1 convert_reduce_fusion.1
  12.6 0.1 copy.28.doc_col_ref
  12.8 0.6 %fusion.2 = s32[]{:T(128)} fusion(s32[8,1]{0,1:T(1,128)S(1)} %reduce-window.4, s32[]{:T(128)S(6)} %sub.9), kind=kLoop, calls=%fused_computation.15 | loop fusion | flops 23 | bytes 40 | tf_op jit(solution)/shard_map/reduce_sum | solution.py:33
  13.4 0.7 %compare_convert_fusion.carried_ref = f32[192,1]{1,0:T(8,128)S(1)} fusion(s32[192,1]{1,0:T(8,128)S(1)} %copy.28.doc_col_ref, s32[]{:T(128)} %fusion.2), kind=kLoop, calls=%fused_computation.6 | loop fusion | flops 384 | bytes 1540 | tf_op jit(solution)/shard_map/convert_element_type | solution.py:284
  14.1 14.8 %shard_map.113 = (bf16[192,2048]{1,0:T(8,128)(2,1)S(1)}, f32[192,2048]{1,0:T(8,128)S(1)}, bf16[16,128,128]{2,1,0:T(8,128)(2,1)S(1)}, f32[16,128,128]{2,1,0:T(8,128)S(1)}) custom-call(bf16[1,192,2048]{2,1,0:T(8,128)(2,1)} %query_ref.3, bf16[1,192,2048]{2,1,0:T(8,128)(2,1)} %key_ref.1, bf16[1,192,2048]{2,1,0:T(8,128)(2,1)} %value_ref.1, ...), custom_call_target="tpu_custom_call" | custom-call | flops 20000000000 | bytes 8000000 | tf_op jit(solution)/shard_map/pallas_call | solution.py:298
  28.9 0.0 copy-start
  28.9 1.1 %copy-done = f32[192,2048]{1,0:T(8,128)} copy-done((f32[192,2048]{1,0:T(8,128)}, f32[192,2048]{1,0:T(8,128)S(1)}, u32[]{:S(2)}) %copy-start) | copy-done | bytes 1572888
  30.0 0.0 copy-start.1
  30.0 0.9 %copy-done.1 = bf16[192,2048]{1,0:T(8,128)(2,1)} copy-done((bf16[192,2048]{1,0:T(8,128)(2,1)}, bf16[192,2048]{1,0:T(8,128)(2,1)S(1)}, u32[]{:S(2)}) %copy-start.1) | copy-done | bytes 786456
  30.9 0.0 copy-start.3
  30.9 0.1 convert_element_type.47
  31.0 1.5 %collective-permute-start = (bf16[16,128,128]{2,1,0:T(8,128)(2,1)S(1)}, bf16[16,128,128]{2,1,0:T(8,128)(2,1)S(1)}, u32[]{:S(2)}, u32[]{:S(2)}) collective-permute-start(bf16[16,128,128]{2,1,0:T(8,128)(2,1)S(1)} %convert_element_type.47), channel_id=1, source_target_pairs={{0,4},{4,8},{8,12},{1,5},{5,9},{9,13},{2,6},{6,10},{10,14},{3,7},{... | collective-permute-start | bytes 1572872 | tf_op jit(solution)/shard_map/ppermute | solution.py:25
  32.5 0.1 eq.36
  32.6 0.1 add_reduce_fusion
  32.7 0.1 iota_add_fusion
  32.8 0.1 broadcast_compare_fusion
  32.9 0.1 convert_reduce_fusion
  33.0 0.1 and_select_fusion.bias_ref
  33.1 0.0 collective-permute-done.3
  33.1 0.0 collective-permute-done.2
  33.1 0.0 copy-done.3
  33.1 1.0 %pad_maximum_fusion = bf16[576,576]{1,0:T(8,128)(2,1)S(1)} fusion(bf16[192,576]{1,0:T(8,128)(2,1)S(1)} %bitcast.17, bf16[192,576]{1,0:T(8,128)(2,1)S(1)} %collective-permute-done.3, bf16[192,576]{1,0:T(8,128)(2,1)} %collective-permute-done.2), kind=kLoop, calls=%fused_computation.3 | loop fusion | flops 1990656 | bytes 1327104 | tf_op jit(solution)/shard_map/concatenate | solution.py:287
  34.2 0.4 fusion.3
  34.6 9.6 %shard_map.116 = bf16[96,2304]{1,0:T(8,128)(2,1)S(1)} custom-call(s32[1]{0:T(128)} %bitcast.6.place_ref, bf16[1,192,9216]{2,1,0:T(8,128)(2,1)} %query_ref.5, bf16[576,640]{1,0:T(8,128)(2,1)S(1)} %get-tuple-element.19.even_ref, bf16[576,640]{1,0:T(8,128)(2,1)S(1)} %get-tuple-element.18.odd_ref, f32[2,96,384]{2,1,0:T(8,128)S(1)} %and_select_fusion.bias_ref, ...), custom_call_target="tpu_custom_call" | custom-call | flops 12000000000 | bytes 16000000 | tf_op jit(solution)/shard_map/pallas_call | solution.py:352
  44.2 1.6 %collective-permute-start.4 = (bf16[96,2304]{1,0:T(8,128)(2,1)S(1)}, bf16[96,2304]{1,0:T(8,128)(2,1)S(1)}, u32[]{:S(2)}, u32[]{:S(2)}) collective-permute-start(bf16[96,2304]{1,0:T(8,128)(2,1)S(1)} %shard_map.116), channel_id=1, source_target_pairs={{0,2},{2,0},{1,3},{3,1},{4,6},{6,4},{5,7},{7,5},{8,10},{10,8},{9,1... | collective-permute-start | bytes 1327112 | tf_op jit(solution)/shard_map/ppermute | solution.py:394
  45.8 0.0 collective-permute-done
  45.8 0.3 fusion
  46.1 2.0 %collective-permute-start.1 = (bf16[16,128,128]{2,1,0:T(8,128)(2,1)S(1)}, bf16[16,128,128]{2,1,0:T(8,128)(2,1)S(1)}, u32[]{:S(2)}, u32[]{:S(2)}) collective-permute-start(bf16[16,128,128]{2,1,0:T(8,128)(2,1)S(1)} %fusion), channel_id=1, source_target_pairs={{0,4},{4,8},{8,12},{1,5},{5,9},{9,13},{2,6},{6,10},{10,14},{3,7},{... | collective-permute-start | bytes 1572872 | tf_op jit(solution)/shard_map/ppermute | solution.py:25
  48.1 9.6 %shard_map.115 = f32[96,2304]{1,0:T(8,128)S(1)} custom-call(s32[1]{0:T(128)} %bitcast.5.place_ref, bf16[1,192,9216]{2,1,0:T(8,128)(2,1)} %query_ref.5, bf16[576,640]{1,0:T(8,128)(2,1)S(1)} %get-tuple-element.19.even_ref, bf16[576,640]{1,0:T(8,128)(2,1)S(1)} %get-tuple-element.18.odd_ref, f32[2,96,384]{2,1,0:T(8,128)S(1)} %and_select_fusion.bias_ref, ...), custom_call_target="tpu_custom_call" | custom-call | flops 12000000000 | bytes 16000000 | tf_op jit(solution)/shard_map/pallas_call | solution.py:352
  57.7 0.0 collective-permute-done.4
  57.7 0.8 %fusion.1 = bf16[1,96,2304]{2,1,0:T(8,128)(2,1)} fusion(f32[96,2304]{1,0:T(8,128)S(1)} %shard_map.115, bf16[96,2304]{1,0:T(8,128)(2,1)S(1)} %collective-permute-done.4), kind=kLoop, calls=%fused_computation.4 | loop fusion | flops 663552 | bytes 1769472 | tf_op jit(solution)/shard_map/broadcast_in_dim | solution.py:421
  58.6 0.0 collective-permute-done.1.state_ref
  58.6 0.0 copy-start.2
  58.6 0.8 %copy-done.2 = bf16[16,128,128]{2,1,0:T(8,128)(2,1)} copy-done((bf16[16,128,128]{2,1,0:T(8,128)(2,1)}, bf16[16,128,128]{2,1,0:T(8,128)(2,1)S(1)}, u32[]{:S(2)}) %copy-start.2) | copy-done | bytes 524312
  59.4 4.0 %shard_map.114 = bf16[1,192,2048]{2,1,0:T(8,128)(2,1)} custom-call(bf16[192,2048]{1,0:T(8,128)(2,1)} %copy-done.1, f32[192,2048]{1,0:T(8,128)} %copy-done, bf16[16,128,128]{2,1,0:T(8,128)(2,1)} %copy-done.2), custom_call_target="tpu_custom_call" | custom-call | flops 100000000 | bytes 4000000 | tf_op jit(solution)/shard_map/pallas_call | solution.py:411
  (4 shorter events, 0.0 us)
Async XLA Ops:
  0.6 32.5 %collective-permute-start.3 = (bf16[192,576]{1,0:T(8,128)(2,1)}, bf16[192,576]{1,0:T(8,128)(2,1)S(1)}, u32[]{:S(2)}, u32[]{:S(2)}) collective-permute-start(bf16[192,576]{1,0:T(8,128)(2,1)} %bitcast.15), channel_id=1, source_target_pairs={{0,4},{4,8},{8,12},{1,5},{5,9},{9,13},{2,6},{6,10},{10,14},{3,7},{... | collective-permute-start | bytes 663560 | tf_op jit(solution)/shard_map/ppermute | solution.py:25
  5.6 27.5 %collective-permute-start.2 = (bf16[192,576]{1,0:T(8,128)(2,1)}, bf16[192,576]{1,0:T(8,128)(2,1)}, u32[]{:S(2)}, u32[]{:S(2)}) collective-permute-start(bf16[192,576]{1,0:T(8,128)(2,1)} %bitcast.16), channel_id=1, source_target_pairs={{0,8},{4,12},{1,9},{5,13},{2,10},{6,14},{3,11},{7,15},{16,24},{20,... | collective-permute-start | bytes 663560 | tf_op jit(solution)/shard_map/ppermute | solution.py:25
  28.9 1.2 %copy-start = (f32[192,2048]{1,0:T(8,128)}, f32[192,2048]{1,0:T(8,128)S(1)}, u32[]{:S(2)}) copy-start(f32[192,2048]{1,0:T(8,128)S(1)} %get-tuple-element.11.local_ref) | copy-start | bytes 4718596
  30.0 0.9 %copy-start.1 = (bf16[192,2048]{1,0:T(8,128)(2,1)}, bf16[192,2048]{1,0:T(8,128)(2,1)S(1)}, u32[]{:S(2)}) copy-start(bf16[192,2048]{1,0:T(8,128)(2,1)S(1)} %get-tuple-element.10.readout_ref) | copy-start | bytes 2359300
  30.9 2.2 %copy-start.3 = (bf16[1,192,576]{2,1,0:T(8,128)(2,1)S(1)}, bf16[1,192,576]{2,1,0:T(8,128)(2,1)}, u32[]{:S(2)}) copy-start(bf16[1,192,576]{2,1,0:T(8,128)(2,1)} %param.16) | copy-start | bytes 663556
  31.0 14.8 %collective-permute-start = (bf16[16,128,128]{2,1,0:T(8,128)(2,1)S(1)}, bf16[16,128,128]{2,1,0:T(8,128)(2,1)S(1)}, u32[]{:S(2)}, u32[]{:S(2)}) collective-permute-start(bf16[16,128,128]{2,1,0:T(8,128)(2,1)S(1)} %convert_element_type.47), channel_id=1, source_target_pairs={{0,4},{4,8},{8,12},{1,5},{5,9},{9,13},{2,6},{6,10},{10,14},{3,7},{... | collective-permute-start | bytes 1572872 | tf_op jit(solution)/shard_map/ppermute | solution.py:25
  44.2 13.5 %collective-permute-start.4 = (bf16[96,2304]{1,0:T(8,128)(2,1)S(1)}, bf16[96,2304]{1,0:T(8,128)(2,1)S(1)}, u32[]{:S(2)}, u32[]{:S(2)}) collective-permute-start(bf16[96,2304]{1,0:T(8,128)(2,1)S(1)} %shard_map.116), channel_id=1, source_target_pairs={{0,2},{2,0},{1,3},{3,1},{4,6},{6,4},{5,7},{7,5},{8,10},{10,8},{9,1... | collective-permute-start | bytes 1327112 | tf_op jit(solution)/shard_map/ppermute | solution.py:394
  46.1 12.5 %collective-permute-start.1 = (bf16[16,128,128]{2,1,0:T(8,128)(2,1)S(1)}, bf16[16,128,128]{2,1,0:T(8,128)(2,1)S(1)}, u32[]{:S(2)}, u32[]{:S(2)}) collective-permute-start(bf16[16,128,128]{2,1,0:T(8,128)(2,1)S(1)} %fusion), channel_id=1, source_target_pairs={{0,4},{4,8},{8,12},{1,5},{5,9},{9,13},{2,6},{6,10},{10,14},{3,7},{... | collective-permute-start | bytes 1572872 | tf_op jit(solution)/shard_map/ppermute | solution.py:25
  58.6 0.8 %copy-start.2 = (bf16[16,128,128]{2,1,0:T(8,128)(2,1)}, bf16[16,128,128]{2,1,0:T(8,128)(2,1)S(1)}, u32[]{:S(2)}) copy-start(bf16[16,128,128]{2,1,0:T(8,128)(2,1)S(1)} %collective-permute-done.1.state_ref) | copy-start | bytes 1572868

commit v4 on v3

--- a/solution.py
+++ b/solution.py
@@ -56,14 +56,13 @@
 
 
 def delta_terms(
+    first_ref,
+    lengths_ref,
     query_ref,
     key_ref,
     value_ref,
     decay_ref,
     strength_ref,
-    doc_col_ref,
-    doc_row_ref,
-    carried_ref,
     readout_ref,
     local_ref,
     transition_ref,
@@ -76,11 +75,22 @@
     row = lax.broadcasted_iota(jnp.int32, (tokens, tokens), 0)
     col = lax.broadcasted_iota(jnp.int32, (tokens, tokens), 1)
     inclusive = jnp.where(row >= col, 1.0, 0.0).astype(jnp.bfloat16)
-    same_doc = doc_col_ref[...] == doc_row_ref[...]
+    first = first_ref[0]
+    pos_col = first + lax.broadcasted_iota(jnp.int32, (tokens, 1), 0)
+    pos_row = first + lax.broadcasted_iota(jnp.int32, (1, tokens), 1)
+    doc_col, doc_row = jnp.zeros_like(pos_col), jnp.zeros_like(pos_row)
+    prev_doc, last_doc, end = jnp.int32(0), jnp.int32(0), jnp.int32(0)
+    for d in range(lengths_ref.shape[0]):
+        end = end + lengths_ref[d]
+        doc_col = doc_col + jnp.where(pos_col >= end, 1, 0)
+        doc_row = doc_row + jnp.where(pos_row >= end, 1, 0)
+        prev_doc = prev_doc + jnp.where(first - 1 >= end, 1, 0)
+        last_doc = last_doc + jnp.where(first + tokens - 1 >= end, 1, 0)
+    same_doc = doc_col == doc_row
     strict = same_doc & (row > col)
     up_to = same_doc & (row >= col)
-    carried = carried_ref[:, 0:1]
-    tail = jnp.where(doc_col_ref[...] == doc_col_ref[tokens - 1 : tokens, :], 1.0, 0.0)
+    carried = jnp.where(doc_col == prev_doc, 1.0, 0.0)
+    tail = jnp.where(doc_col == last_doc, 1.0, 0.0)
     small_row = lax.broadcasted_iota(jnp.int32, (SPAN, SPAN), 0)
     small_col = lax.broadcasted_iota(jnp.int32, (SPAN, SPAN), 1)
     queries, keys, strengths, summed = [], [], [], []
@@ -278,11 +288,9 @@
     hops = min(ctx_count - 1, -(-(longest - 1) // tokens_dev))
     first_pos = ctx_place * tokens_dev
     positions = first_pos + jnp.arange(tokens_dev, dtype=jnp.int32)
-    doc_ends = jnp.cumsum(doc_lengths[0])
+    order = jnp.arange(doc_lengths.shape[1], dtype=jnp.int32)
+    doc_ends = jnp.sum(jnp.where(order[None, :] <= order[:, None], doc_lengths, 0), axis=1)
     doc_ids = doc_index(positions, doc_ends)
-    prev_doc = doc_index(first_pos[None] - 1, doc_ends)
-    carried = (doc_ids == prev_doc).astype(jnp.float32)
-
     window = [from_behind(latents[0], "ctx", by) for by in range(hops, 0, -1)]
     block_rows = jnp.concatenate(window + [latents[0]], axis=0)
 
@@ -291,24 +299,21 @@
     strength = jnp.transpose(
         write_strength[0].reshape(steps, HEADS_STEP, tokens_dev), (0, 2, 1)
     )
-    packed = pl.BlockSpec((1, tokens_dev, lanes_step), lambda i: (0, 0, i))
-    flat = pl.BlockSpec((tokens_dev, lanes_step), lambda i: (0, i))
-    column = pl.BlockSpec((tokens_dev, 1), lambda i: (0, 0))
-    square = pl.BlockSpec((HEADS_STEP, state_dim, state_dim), lambda i: (i, 0, 0))
+    packed = pl.BlockSpec((1, tokens_dev, lanes_step), lambda i, *_: (0, 0, i))
+    flat = pl.BlockSpec((tokens_dev, lanes_step), lambda i, *_: (0, i))
+    square = pl.BlockSpec((HEADS_STEP, state_dim, state_dim), lambda i, *_: (i, 0, 0))
     readout, local_part, transition, offset = pl.pallas_call(
         delta_terms,
-        grid=(steps,),
-        in_specs=[packed] * 4
-        + [
-            pl.BlockSpec((1, tokens_dev, HEADS_STEP), lambda i: (i, 0, 0)),
-            column,
-            pl.BlockSpec((1, tokens_dev), lambda i: (0, 0)),
-            column,
-        ],
-        out_specs=[flat, flat, square, square],
+        grid_spec=pltpu.PrefetchScalarGridSpec(
+            num_scalar_prefetch=2,
+            grid=(steps,),
+            in_specs=[packed] * 4
+            + [pl.BlockSpec((1, tokens_dev, HEADS_STEP), lambda i, *_: (i, 0, 0))],
+            out_specs=[flat, flat, square, square],
+        ),
         out_shape=[
-            jax.ShapeDtypeStruct((tokens_dev, heads_dev * state_dim), jnp.bfloat16),
-            jax.ShapeDtypeStruct((tokens_dev, heads_dev * state_dim), jnp.float32),
+            pltpu.HBM((tokens_dev, heads_dev * state_dim), jnp.bfloat16),
+            pltpu.HBM((tokens_dev, heads_dev * state_dim), jnp.float32),
             jax.ShapeDtypeStruct((heads_dev, state_dim, state_dim), jnp.bfloat16),
             jax.ShapeDtypeStruct((heads_dev, state_dim, state_dim), jnp.float32),
         ],
@@ -317,14 +322,13 @@
             flops=20_000_000_000, bytes_accessed=8_000_000, transcendentals=0
         ),
     )(
+        first_pos[None],
+        doc_lengths[0],
         in_place(kda_query),
         in_place(kda_key),
         in_place(kda_value),
         in_place(log_decay),
         strength,
-        doc_ids[:, None],
-        doc_ids[None, :],
-        carried[:, None],
     )
 
     width = latents.shape[2]

time: 63.9 us -> 60.6 us (0.948)
  other arithmetic: 4.66 us -> 1.69 us
  local copies, waits for them, and re-layouts: 4.41 us -> 2.92 us
  Pallas kernels: 38.1 us -> 39.3 us
    unnamed x8, local copies, waits for them, and re-layouts: 2.84 us -> 1.46 us
    pallas_call x1, Pallas kernels: 14.8 us -> 16 us  [local(): pl.pallas_call(delta_terms, grid_spec=pltpu.PrefetchScalarGridSpec(num_sc...]
    concatenate x1, other arithmetic: 1.01 us -> 0.07 us  [local(): block_rows = jnp.concatenate(window + [latents[0]], axis=0)]
    another operation x1 -> x0, other arithmetic: 0.83 us -> none
    convert_element_type x1 -> x0, other arithmetic: 0.65 us -> none  [local(): carried = (doc_ids == prev_doc).astype(jnp.float32)]
  transfers between devices with their start and end apart: 5 -> 5, of which waited for: 0 -> 0; matrix products, arithmetic and copies ran while one was open for 10% -> 6% of each run, Pallas kernels for 54% -> 59%
where the time goes in v4:
time: 60.6 us; the launch traced here: 60.1 us
  Pallas kernels  39.3 us (65%)
  starting transfers between devices  15.1 us (25%)
  local copies, waits for them, and re-layouts  2.92 us (5%)
  other arithmetic  1.69 us (3%)
  between operations  0.82 us (1%)
    pallas_call x2, Pallas kernels, attention(): pl.pallas_call(functools.partial(latent_attention, width=width, first_key...  19.3 us
    pallas_call x1, Pallas kernels, local(): pl.pallas_call(delta_terms, grid_spec=pltpu.PrefetchScalarGridSpec(num_sc...  16 us
    ppermute x4, starting transfers between devices, from_behind(): return lax.ppermute(value, axis, pairs)  13.6 us
    pallas_call x1, Pallas kernels, local(): pl.pallas_call(delta_readout, grid=(steps,), in_specs=[flat, flat, square...  4.02 us
    ppermute x1, starting transfers between devices, local(): far_part = lax.ppermute(far_part, 'head', [(0, 1), (1, 0)])  1.56 us
    unnamed x8, local copies, waits for them, and re-layouts  1.46 us
  transfers between devices with their start and end apart: 5, of which 0 were waited for; matrix products, arithmetic and copies ran while one was open for 6% of the time, Pallas kernels for 59%

profile of v4, /device:TPU:0, one launch (start us, length us, event | category | flops | bytes accessed | tf_op | source)
XLA Modules:
  0.0 60.1 jit_solution(6318416537448127146)
XLA Ops:
  0.6 4.9 %collective-permute-start.3 = (bf16[192,576]{1,0:T(8,128)(2,1)}, bf16[192,576]{1,0:T(8,128)(2,1)S(1)}, u32[]{:S(2)}, u32[]{:S(2)}) collective-permute-start(bf16[192,576]{1,0:T(8,128)(2,1)} %bitcast.13), channel_id=1, source_target_pairs={{0,4},{4,8},{8,12},{1,5},{5,9},{9,13},{2,6},{6,10},{10,14},{3,7},{... | collective-permute-start | bytes 663560 | tf_op jit(solution)/shard_map/ppermute | solution.py:25
  5.6 4.5 %collective-permute-start.2 = (bf16[192,576]{1,0:T(8,128)(2,1)}, bf16[192,576]{1,0:T(8,128)(2,1)S(1)}, u32[]{:S(2)}, u32[]{:S(2)}) collective-permute-start(bf16[192,576]{1,0:T(8,128)(2,1)} %bitcast.14), channel_id=1, source_target_pairs={{0,8},{4,12},{1,9},{5,13},{2,10},{6,14},{3,11},{7,15},{16,24},{20,... | collective-permute-start | bytes 663560 | tf_op jit(solution)/shard_map/ppermute | solution.py:25
  10.1 0.7 %reshape_squeeze.3 = f32[4,4,192]{2,1,0:T(4,128)S(1)} reshape(f32[1,16,192]{2,1,0:T(8,128)} %param.14) | data formatting | bytes 24576 | tf_op jit(solution)/shard_map/reshape;squeeze | solution.py:300
  10.8 0.2 copy.18
  11.0 0.0 copy-start
  11.0 0.6 %copy-done = s32[1,8]{1,0:T(1,128)S(1)} copy-done((s32[1,8]{1,0:T(1,128)S(1)}, s32[1,8]{1,0:T(1,128)}, u32[]{:S(2)}) %copy-start) | copy-done | bytes 56
  11.7 16.0 %shard_map.113 = (bf16[192,2048]{1,0:T(8,128)(2,1)}, f32[192,2048]{1,0:T(8,128)}, bf16[16,128,128]{2,1,0:T(8,128)(2,1)S(1)}, f32[16,128,128]{2,1,0:T(8,128)S(1)}) custom-call(s32[1]{0:T(128)} %bitcast.first_ref, s32[8]{0:T(128)S(1)} %bitcast.11, bf16[1,192,2048]{2,1,0:T(8,128)(2,1)} %query_ref.3, bf16[1,192,2048]{2,1,0:T(8,128)(2,1)} %key_ref.1, ...), custom_call_target="tpu_custom_call" | custom-call | flops 20000000000 | bytes 8000000 | tf_op jit(solution)/shard_map/pallas_call | solution.py:305
  27.7 0.0 copy-start.1
  27.7 0.0 copy-start.3
  27.7 0.1 convert_element_type.22
  27.8 1.5 %collective-permute-start = (bf16[16,128,128]{2,1,0:T(8,128)(2,1)S(1)}, bf16[16,128,128]{2,1,0:T(8,128)(2,1)S(1)}, u32[]{:S(2)}, u32[]{:S(2)}) collective-permute-start(bf16[16,128,128]{2,1,0:T(8,128)(2,1)S(1)} %convert_element_type.22), channel_id=1, source_target_pairs={{0,4},{4,8},{8,12},{1,5},{5,9},{9,13},{2,6},{6,10},{10,14},{3,7},{... | collective-permute-start | bytes 1572872 | tf_op jit(solution)/shard_map/ppermute | solution.py:25
  29.2 0.0 copy-done.1
  29.3 0.1 select_reduce_fusion
  29.4 0.1 add_reduce_fusion
  29.5 0.1 iota_add_fusion
  29.6 0.1 broadcast_compare_fusion
  29.6 0.1 convert_reduce_fusion.1
  29.7 0.1 eq.19
  29.8 0.1 convert_reduce_fusion
  29.9 0.1 and_select_fusion.bias_ref
  30.1 0.0 collective-permute-done.3
  30.1 0.0 collective-permute-done.2
  30.1 0.0 copy-done.3
  30.1 0.1 pad_maximum_fusion
  30.2 0.4 fusion.2
  30.6 9.6 %shard_map.116 = bf16[96,2304]{1,0:T(8,128)(2,1)S(1)} custom-call(s32[1]{0:T(128)} %bitcast.4.place_ref, bf16[1,192,9216]{2,1,0:T(8,128)(2,1)} %query_ref.5, bf16[576,640]{1,0:T(8,128)(2,1)S(1)} %get-tuple-element.19.even_ref, bf16[576,640]{1,0:T(8,128)(2,1)S(1)} %get-tuple-element.18.odd_ref, f32[2,96,384]{2,1,0:T(8,128)S(1)} %and_select_fusion.bias_ref, ...), custom_call_target="tpu_custom_call" | custom-call | flops 12000000000 | bytes 16000000 | tf_op jit(solution)/shard_map/pallas_call | solution.py:356
  40.3 1.6 %collective-permute-start.4 = (bf16[96,2304]{1,0:T(8,128)(2,1)S(1)}, bf16[96,2304]{1,0:T(8,128)(2,1)S(1)}, u32[]{:S(2)}, u32[]{:S(2)}) collective-permute-start(bf16[96,2304]{1,0:T(8,128)(2,1)S(1)} %shard_map.116), channel_id=1, source_target_pairs={{0,2},{2,0},{1,3},{3,1},{4,6},{6,4},{5,7},{7,5},{8,10},{10,8},{9,1... | collective-permute-start | bytes 1327112 | tf_op jit(solution)/shard_map/ppermute | solution.py:398
  41.8 0.0 collective-permute-done
  41.8 0.3 fusion
  42.1 2.7 %collective-permute-start.1 = (bf16[16,128,128]{2,1,0:T(8,128)(2,1)S(1)}, bf16[16,128,128]{2,1,0:T(8,128)(2,1)S(1)}, u32[]{:S(2)}, u32[]{:S(2)}) collective-permute-start(bf16[16,128,128]{2,1,0:T(8,128)(2,1)S(1)} %fusion), channel_id=1, source_target_pairs={{0,4},{4,8},{8,12},{1,5},{5,9},{9,13},{2,6},{6,10},{10,14},{3,7},{... | collective-permute-start | bytes 1572872 | tf_op jit(solution)/shard_map/ppermute | solution.py:25
  44.8 9.6 %shard_map.115 = f32[96,2304]{1,0:T(8,128)S(1)} custom-call(s32[1]{0:T(128)} %bitcast.3.place_ref, bf16[1,192,9216]{2,1,0:T(8,128)(2,1)} %query_ref.5, bf16[576,640]{1,0:T(8,128)(2,1)S(1)} %get-tuple-element.19.even_ref, bf16[576,640]{1,0:T(8,128)(2,1)S(1)} %get-tuple-element.18.odd_ref, f32[2,96,384]{2,1,0:T(8,128)S(1)} %and_select_fusion.bias_ref, ...), custom_call_target="tpu_custom_call" | custom-call | flops 12000000000 | bytes 16000000 | tf_op jit(solution)/shard_map/pallas_call | solution.py:356
  54.5 0.0 collective-permute-done.4
  54.5 0.8 %fusion.1 = bf16[1,96,2304]{2,1,0:T(8,128)(2,1)} fusion(f32[96,2304]{1,0:T(8,128)S(1)} %shard_map.115, bf16[96,2304]{1,0:T(8,128)(2,1)S(1)} %collective-permute-done.4), kind=kLoop, calls=%fused_computation.4 | loop fusion | flops 663552 | bytes 1769472 | tf_op jit(solution)/shard_map/broadcast_in_dim | solution.py:425
  55.3 0.0 collective-permute-done.1.state_ref
  55.3 0.0 copy-start.2
  55.3 0.8 %copy-done.2 = bf16[16,128,128]{2,1,0:T(8,128)(2,1)} copy-done((bf16[16,128,128]{2,1,0:T(8,128)(2,1)}, bf16[16,128,128]{2,1,0:T(8,128)(2,1)S(1)}, u32[]{:S(2)}) %copy-start.2) | copy-done | bytes 524312
  56.1 4.0 %shard_map.114 = bf16[1,192,2048]{2,1,0:T(8,128)(2,1)} custom-call(bf16[192,2048]{1,0:T(8,128)(2,1)} %get-tuple-element.10.readout_ref, f32[192,2048]{1,0:T(8,128)} %get-tuple-element.11.local_ref, bf16[16,128,128]{2,1,0:T(8,128)(2,1)} %copy-done.2), custom_call_target="tpu_custom_call" | custom-call | flops 100000000 | bytes 4000000 | tf_op jit(solution)/shard_map/pallas_call | solution.py:415
  (4 shorter events, 0.0 us)
Async XLA Ops:
  0.6 29.4 %collective-permute-start.3 = (bf16[192,576]{1,0:T(8,128)(2,1)}, bf16[192,576]{1,0:T(8,128)(2,1)S(1)}, u32[]{:S(2)}, u32[]{:S(2)}) collective-permute-start(bf16[192,576]{1,0:T(8,128)(2,1)} %bitcast.13), channel_id=1, source_target_pairs={{0,4},{4,8},{8,12},{1,5},{5,9},{9,13},{2,6},{6,10},{10,14},{3,7},{... | collective-permute-start | bytes 663560 | tf_op jit(solution)/shard_map/ppermute | solution.py:25
  5.6 24.5 %collective-permute-start.2 = (bf16[192,576]{1,0:T(8,128)(2,1)}, bf16[192,576]{1,0:T(8,128)(2,1)S(1)}, u32[]{:S(2)}, u32[]{:S(2)}) collective-permute-start(bf16[192,576]{1,0:T(8,128)(2,1)} %bitcast.14), channel_id=1, source_target_pairs={{0,8},{4,12},{1,9},{5,13},{2,10},{6,14},{3,11},{7,15},{16,24},{20,... | collective-permute-start | bytes 663560 | tf_op jit(solution)/shard_map/ppermute | solution.py:25
  11.0 0.7 %copy-start = (s32[1,8]{1,0:T(1,128)S(1)}, s32[1,8]{1,0:T(1,128)}, u32[]{:S(2)}) copy-start(s32[1,8]{1,0:T(1,128)} %param.19) | copy-start | bytes 100
  27.7 1.6 %copy-start.1 = (s32[1,8]{1,0:T(1,128)S(1)}, s32[1,8]{1,0:T(1,128)}, u32[]{:S(2)}) copy-start(s32[1,8]{1,0:T(1,128)} %param.19) | copy-start | bytes 100
  27.7 2.4 %copy-start.3 = (bf16[1,192,576]{2,1,0:T(8,128)(2,1)S(1)}, bf16[1,192,576]{2,1,0:T(8,128)(2,1)}, u32[]{:S(2)}) copy-start(bf16[1,192,576]{2,1,0:T(8,128)(2,1)} %param.16) | copy-start | bytes 663556
  27.8 14.1 %collective-permute-start = (bf16[16,128,128]{2,1,0:T(8,128)(2,1)S(1)}, bf16[16,128,128]{2,1,0:T(8,128)(2,1)S(1)}, u32[]{:S(2)}, u32[]{:S(2)}) collective-permute-start(bf16[16,128,128]{2,1,0:T(8,128)(2,1)S(1)} %convert_element_type.22), channel_id=1, source_target_pairs={{0,4},{4,8},{8,12},{1,5},{5,9},{9,13},{2,6},{6,10},{10,14},{3,7},{... | collective-permute-start | bytes 1572872 | tf_op jit(solution)/shard_map/ppermute | solution.py:25
  40.3 14.2 %collective-permute-start.4 = (bf16[96,2304]{1,0:T(8,128)(2,1)S(1)}, bf16[96,2304]{1,0:T(8,128)(2,1)S(1)}, u32[]{:S(2)}, u32[]{:S(2)}) collective-permute-start(bf16[96,2304]{1,0:T(8,128)(2,1)S(1)} %shard_map.116), channel_id=1, source_target_pairs={{0,2},{2,0},{1,3},{3,1},{4,6},{6,4},{5,7},{7,5},{8,10},{10,8},{9,1... | collective-permute-start | bytes 1327112 | tf_op jit(solution)/shard_map/ppermute | solution.py:398
  42.1 13.2 %collective-permute-start.1 = (bf16[16,128,128]{2,1,0:T(8,128)(2,1)S(1)}, bf16[16,128,128]{2,1,0:T(8,128)(2,1)S(1)}, u32[]{:S(2)}, u32[]{:S(2)}) collective-permute-start(bf16[16,128,128]{2,1,0:T(8,128)(2,1)S(1)} %fusion), channel_id=1, source_target_pairs={{0,4},{4,8},{8,12},{1,5},{5,9},{9,13},{2,6},{6,10},{10,14},{3,7},{... | collective-permute-start | bytes 1572872 | tf_op jit(solution)/shard_map/ppermute | solution.py:25
  55.3 0.8 %copy-start.2 = (bf16[16,128,128]{2,1,0:T(8,128)(2,1)}, bf16[16,128,128]{2,1,0:T(8,128)(2,1)S(1)}, u32[]{:S(2)}) copy-start(bf16[16,128,128]{2,1,0:T(8,128)(2,1)S(1)} %collective-permute-done.1.state_ref) | copy-start | bytes 1572868

commit v5 on v4

--- a/solution.py
+++ b/solution.py
@@ -189,11 +189,16 @@
 
 def delta_readout(readout_ref, local_ref, state_ref, out_ref):
     state_dim = state_ref.shape[1]
-    for h in range(state_ref.shape[0]):
+    first_head = pl.program_id(0) * HEADS_STEP
+    for h in range(HEADS_STEP):
         lanes = slice(h * state_dim, (h + 1) * state_dim)
         out_ref[0, :, lanes] = (
             local_ref[:, lanes]
-            + jnp.dot(readout_ref[:, lanes], state_ref[h], preferred_element_type=jnp.float32)
+            + jnp.dot(
+                readout_ref[:, lanes],
+                state_ref[first_head + h],
+                preferred_element_type=jnp.float32,
+            )
         ).astype(out_ref.dtype)
 
 
@@ -415,13 +420,13 @@
     kda_out = pl.pallas_call(
         delta_readout,
         grid=(steps,),
-        in_specs=[flat, flat, square],
+        in_specs=[flat, flat, pl.BlockSpec(memory_space=pltpu.VMEM)],
         out_specs=packed,
         out_shape=jax.ShapeDtypeStruct((1, tokens_dev, heads_dev * state_dim), jnp.bfloat16),
         cost_estimate=pl.CostEstimate(
             flops=100_000_000, bytes_accessed=4_000_000, transcendentals=0
         ),
-    )(readout, local_part, inbound_state)
+    )(readout, local_part, pltpu.with_memory_space_constraint(inbound_state, pltpu.VMEM))
     return (kda_out, mixed[None])
 
 

time: 60.6 us -> 59.7 us (0.985)
  local copies, waits for them, and re-layouts: 2.92 us -> 2.11 us
    unnamed x8 -> x6, local copies, waits for them, and re-layouts: 1.46 us -> 0.66 us
where the time goes in v5:
time: 59.7 us; the launch traced here: 59.3 us
  Pallas kernels  39.2 us (66%)
  starting transfers between devices  15.1 us (25%)
  local copies, waits for them, and re-layouts  2.11 us (4%)
  other arithmetic  1.69 us (3%)
  between operations  0.82 us (1%)
    pallas_call x2, Pallas kernels, attention(): pl.pallas_call(functools.partial(latent_attention, width=width, first_key...  19.3 us
    pallas_call x1, Pallas kernels, local(): pl.pallas_call(delta_terms, grid_spec=pltpu.PrefetchScalarGridSpec(num_sc...  16 us
    ppermute x4, starting transfers between devices, from_behind(): return lax.ppermute(value, axis, pairs)  13.6 us
    pallas_call x1, Pallas kernels, local(): pl.pallas_call(delta_readout, grid=(steps,), in_specs=[flat, flat, pl.Blo...  3.97 us
    ppermute x1, starting transfers between devices, local(): far_part = lax.ppermute(far_part, 'head', [(0, 1), (1, 0)])  1.56 us
  transfers between devices with their start and end apart: 5, of which 0 were waited for; matrix products, arithmetic and copies ran while one was open for 6% of the time, Pallas kernels for 59%

profile of v5, /device:TPU:0, one launch (start us, length us, event | category | flops | bytes accessed | tf_op | source)
XLA Modules:
  0.0 59.3 jit_solution(8796536788743901915)
XLA Ops:
  0.6 4.9 %collective-permute-start.3 = (bf16[192,576]{1,0:T(8,128)(2,1)}, bf16[192,576]{1,0:T(8,128)(2,1)S(1)}, u32[]{:S(2)}, u32[]{:S(2)}) collective-permute-start(bf16[192,576]{1,0:T(8,128)(2,1)} %bitcast.13), channel_id=1, source_target_pairs={{0,4},{4,8},{8,12},{1,5},{5,9},{9,13},{2,6},{6,10},{10,14},{3,7},{... | collective-permute-start | bytes 663560 | tf_op jit(solution)/shard_map/ppermute | solution.py:25
  5.6 4.5 %collective-permute-start.2 = (bf16[192,576]{1,0:T(8,128)(2,1)}, bf16[192,576]{1,0:T(8,128)(2,1)S(1)}, u32[]{:S(2)}, u32[]{:S(2)}) collective-permute-start(bf16[192,576]{1,0:T(8,128)(2,1)} %bitcast.14), channel_id=1, source_target_pairs={{0,8},{4,12},{1,9},{5,13},{2,10},{6,14},{3,11},{7,15},{16,24},{20,... | collective-permute-start | bytes 663560 | tf_op jit(solution)/shard_map/ppermute | solution.py:25
  10.1 0.7 %reshape_squeeze.3 = f32[4,4,192]{2,1,0:T(4,128)S(1)} reshape(f32[1,16,192]{2,1,0:T(8,128)} %param.14) | data formatting | bytes 24576 | tf_op jit(solution)/shard_map/reshape;squeeze | solution.py:305
  10.8 0.2 copy.18
  11.0 0.0 copy-start
  11.0 0.6 %copy-done = s32[1,8]{1,0:T(1,128)S(1)} copy-done((s32[1,8]{1,0:T(1,128)S(1)}, s32[1,8]{1,0:T(1,128)}, u32[]{:S(2)}) %copy-start) | copy-done | bytes 56
  11.7 16.0 %shard_map.113 = (bf16[192,2048]{1,0:T(8,128)(2,1)}, f32[192,2048]{1,0:T(8,128)}, bf16[16,128,128]{2,1,0:T(8,128)(2,1)S(1)}, f32[16,128,128]{2,1,0:T(8,128)S(1)}) custom-call(s32[1]{0:T(128)} %bitcast.first_ref, s32[8]{0:T(128)S(1)} %bitcast.11, bf16[1,192,2048]{2,1,0:T(8,128)(2,1)} %query_ref.3, bf16[1,192,2048]{2,1,0:T(8,128)(2,1)} %key_ref.1, ...), custom_call_target="tpu_custom_call" | custom-call | flops 20000000000 | bytes 8000000 | tf_op jit(solution)/shard_map/pallas_call | solution.py:310
  27.7 0.0 copy-start.1
  27.7 0.0 copy-start.2
  27.7 0.1 convert_element_type.22
  27.8 1.5 %collective-permute-start = (bf16[16,128,128]{2,1,0:T(8,128)(2,1)S(1)}, bf16[16,128,128]{2,1,0:T(8,128)(2,1)S(1)}, u32[]{:S(2)}, u32[]{:S(2)}) collective-permute-start(bf16[16,128,128]{2,1,0:T(8,128)(2,1)S(1)} %convert_element_type.22), channel_id=1, source_target_pairs={{0,4},{4,8},{8,12},{1,5},{5,9},{9,13},{2,6},{6,10},{10,14},{3,7},{... | collective-permute-start | bytes 1572872 | tf_op jit(solution)/shard_map/ppermute | solution.py:25
  29.2 0.0 copy-done.1
  29.3 0.1 select_reduce_fusion
  29.4 0.1 add_reduce_fusion
  29.5 0.1 iota_add_fusion
  29.6 0.1 broadcast_compare_fusion
  29.6 0.1 convert_reduce_fusion.1
  29.7 0.1 eq.19
  29.8 0.1 convert_reduce_fusion
  29.9 0.1 and_select_fusion.bias_ref
  30.1 0.0 collective-permute-done.3
  30.1 0.0 collective-permute-done.2
  30.1 0.0 copy-done.2
  30.1 0.1 pad_maximum_fusion
  30.2 0.4 fusion.2
  30.6 9.6 %shard_map.116 = bf16[96,2304]{1,0:T(8,128)(2,1)S(1)} custom-call(s32[1]{0:T(128)} %bitcast.4.place_ref, bf16[1,192,9216]{2,1,0:T(8,128)(2,1)} %query_ref.5, bf16[576,640]{1,0:T(8,128)(2,1)S(1)} %get-tuple-element.19.even_ref, bf16[576,640]{1,0:T(8,128)(2,1)S(1)} %get-tuple-element.18.odd_ref, f32[2,96,384]{2,1,0:T(8,128)S(1)} %and_select_fusion.bias_ref, ...), custom_call_target="tpu_custom_call" | custom-call | flops 12000000000 | bytes 16000000 | tf_op jit(solution)/shard_map/pallas_call | solution.py:361
  40.3 1.6 %collective-permute-start.4 = (bf16[96,2304]{1,0:T(8,128)(2,1)S(1)}, bf16[96,2304]{1,0:T(8,128)(2,1)S(1)}, u32[]{:S(2)}, u32[]{:S(2)}) collective-permute-start(bf16[96,2304]{1,0:T(8,128)(2,1)S(1)} %shard_map.116), channel_id=1, source_target_pairs={{0,2},{2,0},{1,3},{3,1},{4,6},{6,4},{5,7},{7,5},{8,10},{10,8},{9,1... | collective-permute-start | bytes 1327112 | tf_op jit(solution)/shard_map/ppermute | solution.py:403
  41.8 0.0 collective-permute-done
  41.8 0.3 fusion
  42.1 2.7 %collective-permute-start.1 = (bf16[16,128,128]{2,1,0:T(8,128)(2,1)S(1)}, bf16[16,128,128]{2,1,0:T(8,128)(2,1)S(1)}, u32[]{:S(2)}, u32[]{:S(2)}) collective-permute-start(bf16[16,128,128]{2,1,0:T(8,128)(2,1)S(1)} %fusion), channel_id=1, source_target_pairs={{0,4},{4,8},{8,12},{1,5},{5,9},{9,13},{2,6},{6,10},{10,14},{3,7},{... | collective-permute-start | bytes 1572872 | tf_op jit(solution)/shard_map/ppermute | solution.py:25
  44.8 9.6 %shard_map.115 = f32[96,2304]{1,0:T(8,128)S(1)} custom-call(s32[1]{0:T(128)} %bitcast.3.place_ref, bf16[1,192,9216]{2,1,0:T(8,128)(2,1)} %query_ref.5, bf16[576,640]{1,0:T(8,128)(2,1)S(1)} %get-tuple-element.19.even_ref, bf16[576,640]{1,0:T(8,128)(2,1)S(1)} %get-tuple-element.18.odd_ref, f32[2,96,384]{2,1,0:T(8,128)S(1)} %and_select_fusion.bias_ref, ...), custom_call_target="tpu_custom_call" | custom-call | flops 12000000000 | bytes 16000000 | tf_op jit(solution)/shard_map/pallas_call | solution.py:361
  54.5 0.0 collective-permute-done.4
  54.5 0.8 %fusion.1 = bf16[1,96,2304]{2,1,0:T(8,128)(2,1)} fusion(f32[96,2304]{1,0:T(8,128)S(1)} %shard_map.115, bf16[96,2304]{1,0:T(8,128)(2,1)S(1)} %collective-permute-done.4), kind=kLoop, calls=%fused_computation.4 | loop fusion | flops 663552 | bytes 1769472 | tf_op jit(solution)/shard_map/broadcast_in_dim | solution.py:430
  55.3 0.0 collective-permute-done.1.state_ref
  55.3 4.0 %shard_map.114 = bf16[1,192,2048]{2,1,0:T(8,128)(2,1)} custom-call(bf16[192,2048]{1,0:T(8,128)(2,1)} %get-tuple-element.10.readout_ref, f32[192,2048]{1,0:T(8,128)} %get-tuple-element.11.local_ref, bf16[16,128,128]{2,1,0:T(8,128)(2,1)S(1)} %collective-permute-done.1.state_ref), custom_call_target="tpu_custom_call" | custom-call | flops 100000000 | bytes 4000000 | tf_op jit(solution)/shard_map/pallas_call | solution.py:420
  (4 shorter events, 0.0 us)
Async XLA Ops:
  0.6 29.4 %collective-permute-start.3 = (bf16[192,576]{1,0:T(8,128)(2,1)}, bf16[192,576]{1,0:T(8,128)(2,1)S(1)}, u32[]{:S(2)}, u32[]{:S(2)}) collective-permute-start(bf16[192,576]{1,0:T(8,128)(2,1)} %bitcast.13), channel_id=1, source_target_pairs={{0,4},{4,8},{8,12},{1,5},{5,9},{9,13},{2,6},{6,10},{10,14},{3,7},{... | collective-permute-start | bytes 663560 | tf_op jit(solution)/shard_map/ppermute | solution.py:25
  5.6 24.5 %collective-permute-start.2 = (bf16[192,576]{1,0:T(8,128)(2,1)}, bf16[192,576]{1,0:T(8,128)(2,1)S(1)}, u32[]{:S(2)}, u32[]{:S(2)}) collective-permute-start(bf16[192,576]{1,0:T(8,128)(2,1)} %bitcast.14), channel_id=1, source_target_pairs={{0,8},{4,12},{1,9},{5,13},{2,10},{6,14},{3,11},{7,15},{16,24},{20,... | collective-permute-start | bytes 663560 | tf_op jit(solution)/shard_map/ppermute | solution.py:25
  11.0 0.7 %copy-start = (s32[1,8]{1,0:T(1,128)S(1)}, s32[1,8]{1,0:T(1,128)}, u32[]{:S(2)}) copy-start(s32[1,8]{1,0:T(1,128)} %param.19) | copy-start | bytes 100
  27.7 1.6 %copy-start.1 = (s32[1,8]{1,0:T(1,128)S(1)}, s32[1,8]{1,0:T(1,128)}, u32[]{:S(2)}) copy-start(s32[1,8]{1,0:T(1,128)} %param.19) | copy-start | bytes 100
  27.7 2.4 %copy-start.2 = (bf16[1,192,576]{2,1,0:T(8,128)(2,1)S(1)}, bf16[1,192,576]{2,1,0:T(8,128)(2,1)}, u32[]{:S(2)}) copy-start(bf16[1,192,576]{2,1,0:T(8,128)(2,1)} %param.16) | copy-start | bytes 663556
  27.8 14.1 %collective-permute-start = (bf16[16,128,128]{2,1,0:T(8,128)(2,1)S(1)}, bf16[16,128,128]{2,1,0:T(8,128)(2,1)S(1)}, u32[]{:S(2)}, u32[]{:S(2)}) collective-permute-start(bf16[16,128,128]{2,1,0:T(8,128)(2,1)S(1)} %convert_element_type.22), channel_id=1, source_target_pairs={{0,4},{4,8},{8,12},{1,5},{5,9},{9,13},{2,6},{6,10},{10,14},{3,7},{... | collective-permute-start | bytes 1572872 | tf_op jit(solution)/shard_map/ppermute | solution.py:25
  40.3 14.2 %collective-permute-start.4 = (bf16[96,2304]{1,0:T(8,128)(2,1)S(1)}, bf16[96,2304]{1,0:T(8,128)(2,1)S(1)}, u32[]{:S(2)}, u32[]{:S(2)}) collective-permute-start(bf16[96,2304]{1,0:T(8,128)(2,1)S(1)} %shard_map.116), channel_id=1, source_target_pairs={{0,2},{2,0},{1,3},{3,1},{4,6},{6,4},{5,7},{7,5},{8,10},{10,8},{9,1... | collective-permute-start | bytes 1327112 | tf_op jit(solution)/shard_map/ppermute | solution.py:403
  42.1 13.2 %collective-permute-start.1 = (bf16[16,128,128]{2,1,0:T(8,128)(2,1)S(1)}, bf16[16,128,128]{2,1,0:T(8,128)(2,1)S(1)}, u32[]{:S(2)}, u32[]{:S(2)}) collective-permute-start(bf16[16,128,128]{2,1,0:T(8,128)(2,1)S(1)} %fusion), channel_id=1, source_target_pairs={{0,4},{4,8},{8,12},{1,5},{5,9},{9,13},{2,6},{6,10},{10,14},{3,7},{... | collective-permute-start | bytes 1572872 | tf_op jit(solution)/shard_map/ppermute | solution.py:25
